TPU v7x, 512 devices: a whole 4x4x16 slice. The times are simulated.
512 devices in a mesh: fsdp: 64 (over x, y, z_hi, core), ctx: 8 (over z_lo).
Axes of the slice: x: 4, y: 4, z: 16 (z_hi: 2, z_lo: 8; z = z_hi * 8 + z_lo), core: 2. Of those that a mesh axis runs over, the one named last changes fastest.
Arguments:
- token_ids: int32 [1024], P('ctx'), may hold values from 0 to 511
- embed: bfloat16 [512, 8192], P(None, 'fsdp'), may hold values from -6 to 6
- w_in: bfloat16 [8192, 3, 8192], P('ctx', None, 'fsdp'), may hold values from -0.1875 to 0.1875
- taps: float32 [7, 3, 8192], P(None, None, 'fsdp'), may hold values from -2 to 2
- rates: float32 [16, 8192], P(None, 'fsdp'), may hold values from 9.765625e-05 to 0.08, as said below
- residues: float32 [16, 8192], P(None, 'fsdp'), may hold values from -0.15 to 0.15
- cotangent: bfloat16 [1024, 8192], P('ctx', 'fsdp'), may hold values from -6 to 6
Outputs:
- mixed: bfloat16 [1024, 8192], P('ctx', 'fsdp')
- input_grad: bfloat16 [1024, 8192], P('ctx', 'fsdp')
Inputs may be any that keep to these rules, and one draw needn't show every extreme that they name: `rates`: every rate lies between 0.1 / 1024 and 0.08.
All inputs are finite; a program needn't handle non-finite values.
Results may differ from a plain program's by a relative error of at most 0.0064.
Values may be sent and summed in bfloat16 or wider, within the bound.
A program may use at most 64 MiB of HBM per device.

v0:
```python
import jax
import jax.numpy as jnp
from jax import lax
from jax.sharding import PartitionSpec as P


def from_behind(shard, axis, by):
    count = lax.axis_size(axis)
    pairs = [(i, i + by) for i in range(count) if 0 <= i + by < count]
    return lax.ppermute(shard, axis, pairs)


def pair_combine(earlier, later):
    return (earlier[0] * later[0], later[0] * earlier[1] + later[1])


def modal_states(drive, step_decay):
    tok_count = drive.shape[0]
    factors = jnp.broadcast_to(step_decay[None], (tok_count,) + step_decay.shape)
    inputs = jnp.broadcast_to(drive[:, None, :], factors.shape)
    return lax.associative_scan(pair_combine, (factors, inputs), axis=0)[1]


def short_filter(extended, taps, tok_count):
    rim_width = taps.shape[0] - 1
    filtered = taps[0] * extended[rim_width : rim_width + tok_count]
    for shift_lag in range(1, rim_width + 1):
        filtered = (
            filtered
            + taps[shift_lag] * extended[rim_width - shift_lag : rim_width - shift_lag + tok_count]
        )
    return filtered


def short_adjoint(extended, taps, tok_count):
    rim_width = taps.shape[0] - 1
    result = taps[0] * extended[:tok_count]
    for shift_lag in range(1, rim_width + 1):
        result = result + taps[shift_lag] * extended[shift_lag : shift_lag + tok_count]
    return result


def carry_forward(block_decay, leaving):
    zero_state = jnp.zeros_like(leaving)

    def relay_step(turn_index, incoming):
        return from_behind(block_decay * incoming + leaving, "ctx", 1)

    return lax.fori_loop(0, lax.axis_size("ctx") - 1, relay_step, zero_state)


def carry_backward(block_decay, leaving):
    zero_state = jnp.zeros_like(leaving)

    def relay_step(turn_index, incoming):
        return from_behind(block_decay * incoming + leaving, "ctx", -1)

    return lax.fori_loop(0, lax.axis_size("ctx") - 1, relay_step, zero_state)


def on_device(token_ids, embed, w_in, taps, rates, residues, cotangent):
    tok_count = token_ids.shape[0]
    vocab_size = embed.shape[0]
    chan_width = embed.shape[1]
    rim_width = taps.shape[0] - 1
    onehot = (
        token_ids[:, None] == lax.broadcasted_iota(jnp.int32, (tok_count, vocab_size), 1)
    ).astype(jnp.bfloat16)
    embedded = jnp.dot(onehot, embed, preferred_element_type=jnp.float32).astype(jnp.bfloat16)
    features = lax.all_gather(embedded, "fsdp", axis=1, tiled=True)
    feat_width = features.shape[1]
    whole_w = lax.all_gather(w_in, "ctx", axis=0, tiled=True).reshape(feat_width, 3 * chan_width)
    projected = jnp.dot(features, whole_w, preferred_element_type=jnp.float32)
    stored = lax.optimization_barrier(
        projected.astype(jnp.bfloat16).reshape(tok_count, 3, chan_width)
    )
    before = from_behind(stored[tok_count - rim_width :], "ctx", 1)
    extended = jnp.concatenate([before, stored], axis=0).astype(jnp.float32)
    filtered = short_filter(extended, taps, tok_count)
    query_part = filtered[:, 0]
    key_part = filtered[:, 1]
    value_part = filtered[:, 2]
    drive = key_part * value_part
    step_decay = jnp.exp(-rates)
    block_decay = jnp.exp(-rates * tok_count)
    local_states = modal_states(drive, step_decay)
    entering = carry_forward(block_decay, local_states[tok_count - 1])
    offsets = lax.broadcasted_iota(jnp.float32, (tok_count, 1, 1), 0)
    states = local_states + jnp.exp(-rates[None] * (offsets + 1.0)) * entering[None]
    long_out = jnp.sum(residues[None] * states, axis=1)
    mixed = (query_part * long_out).astype(jnp.bfloat16)
    incoming = cotangent.astype(jnp.float32)
    grad_long = incoming * query_part
    grad_query = incoming * long_out
    back_states = jnp.flip(modal_states(jnp.flip(grad_long, 0), step_decay), 0)
    beyond = carry_backward(block_decay, back_states[0])
    adjoint = back_states + jnp.exp(-rates[None] * (tok_count - offsets)) * beyond[None]
    grad_drive = jnp.sum(residues[None] * adjoint, axis=1)
    grad_filtered = jnp.stack([grad_query, grad_drive * value_part, grad_drive * key_part], axis=1)
    after = from_behind(grad_filtered[:rim_width], "ctx", -1)
    ext_grad = jnp.concatenate([grad_filtered, after], axis=0)
    grad_stored = short_adjoint(ext_grad, taps, tok_count).astype(jnp.bfloat16)
    grad_rows = grad_stored.reshape(tok_count, 3 * chan_width)
    own_rows = lax.psum_scatter(
        lax.dot_general(
            whole_w, grad_rows, (((1,), (1,)), ((), ())), preferred_element_type=jnp.float32
        ),
        "fsdp",
        scatter_dimension=0,
        tiled=True,
    )
    return (mixed, own_rows.T.astype(jnp.bfloat16))


def solution(mesh):
    in_specs = (
        P("ctx"),
        P(None, "fsdp"),
        P("ctx", None, "fsdp"),
        P(None, None, "fsdp"),
        P(None, "fsdp"),
        P(None, "fsdp"),
        P("ctx", "fsdp"),
    )
    out_specs = (P("ctx", "fsdp"), P("ctx", "fsdp"))
    return jax.shard_map(
        on_device, mesh=mesh, in_specs=in_specs, out_specs=out_specs, check_vma=False
    )
```

profile of v0, /device:TPU:1, one launch (start us, length us, event | category | flops | bytes accessed | tf_op | source)
XLA Modules:
  0.0 1017.9 jit_solution(2259740171659935697)
XLA Ops:
  8.1 1.5 convolution_convert_fusion.1
  9.7 1.0 fusion.44
  10.7 1.3 fusion.45
  12.0 146.5 %all-gather.5.cloned.1.call-done = bf16[8192,3,128]{2,0,1:T(8,128)(2,1)} async-done(((bf16[1024,3,128]{2,0,1:T(8,128)(2,1)}), bf16[8192,3,128]{2,0,1:T(8,128)(2,1)}) %all-gather.5.cloned.1.call-update) | async-done | bytes 6291472 | tf_op jit(solution)/shard_map/all_gather | solution.py:72
  158.5 8.7 copy.33
  167.2 109.1 %all-gather.3.cloned.1.call-done = bf16[128,8192]{1,0:T(8,128)(2,1)} async-done(((bf16[128,128]{1,0:T(8,128)(2,1)}), bf16[128,8192]{1,0:T(8,128)(2,1)}) %all-gather.3.cloned.1.call-update) | async-done | bytes 2097168 | tf_op jit(solution)/shard_map/all_gather | solution.py:70
  276.2 5.4 convolution_convert_fusion
  281.9 1.3 collective-permute-start.2
  287.8 0.9 add.289
  288.6 1.0 fusion.1
  290.2 22.4 %pad.113 = f32[128,16,128]{2,1,0:T(8,128)S(1)} pad(f32[64,16,128]{2,1,0:T(8,128)} %add.289, f32[]{:T(128)} %constant.12.clone.1), padding=1_0_1x0_0_0x0_0_0 | pad | bytes 1572868 | tf_op jit(solution)/shard_map/pad | solution.py:21
  312.6 1.1 add.291
  314.3 1.9 pad_maximum_fusion
  316.2 22.4 %pad.98 = f32[128,16,128]{2,1,0:T(8,128)S(1)} pad(f32[64,16,128]{2,1,0:T(8,128)} %pad_maximum_fusion, f32[]{:T(128)} %constant.12.clone.1), padding=0_1_1x0_0_0x0_0_0 | pad | bytes 1572868 | tf_op jit(solution)/shard_map/pad | solution.py:21
  338.6 31.1 %while.21 = (s32[]{:T(128)}, f32[16,128]{1,0:T(8,128)S(1)}, f32[16,128]{1,0:T(8,128)S(1)}, f32[16,128]{1,0:T(8,128)S(1)}, s32[]{:T(128)}) while((s32[]{:T(128)}, f32[16,128]{1,0:T(8,128)S(1)}, f32[16,128]{1,0:T(8,128)S(1)}, f32[16,128]{1,0:T(8,128)S(1)}, s32[]{:T(128)}) %tuple.74), condition=%wide.region_4.5_spmd, body=%wide.region_3.4_spmd.sunk | while | flops 4098 | bytes 65637 | solution.py:58
  338.6 1.3 collective-permute-start.1
  339.9 3.3 collective-permute-done.1
  343.2 1.3 collective-permute-start.1
  344.5 3.1 collective-permute-done.1
  347.6 1.3 collective-permute-start.1
  348.9 3.1 collective-permute-done.1
  352.0 1.3 collective-permute-start.1
  353.3 3.1 collective-permute-done.1
  356.4 1.3 collective-permute-start.1
  357.7 3.1 collective-permute-done.1
  360.8 1.3 collective-permute-start.1
  362.1 3.1 collective-permute-done.1
  365.2 1.3 collective-permute-start.1
  366.5 3.2 collective-permute-done.1
  369.6 35.5 %while.20 = (s32[]{:T(128)}, f32[16,128]{1,0:T(8,128)S(1)}, f32[16,128]{1,0:T(8,128)S(1)}, f32[16,128]{1,0:T(8,128)S(1)}, s32[]{:T(128)}) while((s32[]{:T(128)}, f32[16,128]{1,0:T(8,128)S(1)}, f32[16,128]{1,0:T(8,128)S(1)}, f32[16,128]{1,0:T(8,128)S(1)}, s32[]{:T(128)}) %tuple.86), condition=%wide.region_1.0_spmd, body=%wide.region_0.0_spmd.sunk | while | flops 4098 | bytes 65637 | solution.py:49
  369.6 4.9 collective-permute-start
  375.4 4.2 collective-permute-start
  379.6 0.8 collective-permute-done
  380.3 4.6 collective-permute-start
  384.9 0.8 collective-permute-done
  385.7 3.6 collective-permute-start
  389.3 0.8 collective-permute-done
  390.1 3.6 collective-permute-start
  393.7 0.8 collective-permute-done
  394.5 4.3 collective-permute-start
  398.8 0.8 collective-permute-done
  399.6 4.8 collective-permute-start
  405.2 1.5 multiply_reduce_fusion
  407.4 1.3 collective-permute-start.3
  408.7 4.6 collective-permute-done.3
  413.3 7.1 convolution_bitcast_fusion
  420.4 589.5 %reduce-scatter.2.cloned.1.call-done = f32[128,128]{0,1:T(8,128)} async-done(((f32[8192,128]{0,1:T(8,128)}), f32[128,128]{0,1:T(8,128)}) %reduce-scatter.2.cloned.1.call-update) | async-done | bytes 65552 | tf_op jit(solution)/shard_map/reduce_scatter | solution.py:104
  1009.9 1.5 convert_bitcast_fusion
  (141 shorter events, 8.6 us)
Async XLA Ops:
  7.2 0.9 copy-start
  7.2 151.3 %all-gather.5.cloned.1.call-start = ((), (), s32[]{:S(2)}) async-start(), calls=%async_computation.2 | async-start | bytes 7077888 | tf_op jit(solution)/shard_map/all_gather | solution.py:72
  7.9 268.3 %all-gather.3.cloned.1.call-start = ((), (), s32[]{:S(2)}) async-start(), calls=%async_computation.1 | async-start | bytes 2129920 | tf_op jit(solution)/shard_map/all_gather | solution.py:70
  9.6 1000.3 %reduce-scatter.2.cloned.1.call-start = ((), (), s32[]{:S(2)}) async-start(), calls=%async_computation.3 | async-start | bytes 4259840 | tf_op jit(solution)/shard_map/reduce_scatter | solution.py:104
  10.7 273.4 %copy-start.4 = (f32[3,128]{1,0:T(4,128)}, f32[3,128]{1,0:T(4,128)S(1)}, u32[]{:S(2)}) copy-start(f32[3,128]{1,0:T(4,128)S(1)} %get-tuple-element.123) | copy-start | bytes 4612
  10.7 273.4 %copy-start.5 = (f32[3,128]{1,0:T(4,128)}, f32[3,128]{1,0:T(4,128)S(1)}, u32[]{:S(2)}) copy-start(f32[3,128]{1,0:T(4,128)S(1)} %get-tuple-element.124) | copy-start | bytes 4612
  10.7 273.3 %copy-start.6 = (f32[3,128]{1,0:T(4,128)}, f32[3,128]{1,0:T(4,128)S(1)}, u32[]{:S(2)}) copy-start(f32[3,128]{1,0:T(4,128)S(1)} %get-tuple-element.125) | copy-start | bytes 4612
  10.7 273.3 %copy-start.7 = (f32[3,128]{1,0:T(4,128)}, f32[3,128]{1,0:T(4,128)S(1)}, u32[]{:S(2)}) copy-start(f32[3,128]{1,0:T(4,128)S(1)} %get-tuple-element.126) | copy-start | bytes 4612
  167.2 117.1 %copy-start.3 = (bf16[128,128]{1,0:T(8,128)(2,1)S(1)}, bf16[128,128]{1,0:T(8,128)(2,1)}, u32[]{:S(2)}) copy-start(bf16[128,128]{1,0:T(8,128)(2,1)} %param.17) | copy-start | bytes 98308
  276.2 8.5 copy-start.2
  281.9 2.1 collective-permute-start.2
  283.8 0.9 copy-start.8
  313.7 91.5 %copy-start.1 = (f32[128,16,128]{2,1,0:T(8,128)S(1)}, f32[128,16,128]{2,1,0:T(8,128)}, u32[]{:S(2)}) copy-start(f32[128,16,128]{2,1,0:T(8,128)} %add.291) | copy-start | bytes 3145732
  338.6 4.6 collective-permute-start.1
  343.2 4.4 collective-permute-start.1
  347.6 4.4 collective-permute-start.1
  352.0 4.4 collective-permute-start.1
  356.4 4.4 collective-permute-start.1
  360.8 4.4 collective-permute-start.1
  365.2 4.4 collective-permute-start.1
  369.6 5.7 collective-permute-start
  375.4 5.0 collective-permute-start
  380.3 5.3 collective-permute-start
  385.7 4.4 collective-permute-start
  390.1 4.4 collective-permute-start
  394.5 5.1 collective-permute-start
  399.6 5.6 collective-permute-start
  407.4 5.9 collective-permute-start.3
Sparse Core Ops, SparseCore 0:
  10.1 148.3 all-gather.4
  163.2 112.9 all-gather.2
  420.6 589.3 reduce-scatter.1
where the time goes:
time: 1030 us; the launch traced here: 1020 us
  waiting for transfers between devices  878 us (85%)
  local copies, waits for them, and re-layouts  58 us (6%)
  starting transfers between devices  41.7 us (4%)
  between operations  14.5 us (1%)
  matrix products  14 us (1%)
  other arithmetic  11.6 us (1%)
    reduce_scatter x1, waiting for transfers between devices, on_device(): lax.psum_scatter(lax.dot_general(whole_w, grad_rows, (((1,), (1,)), ((),...  589 us
    all_gather x1, waiting for transfers between devices, on_device(): lax.all_gather(w_in, 'ctx', axis=0, tiled=True)  146 us
    all_gather x1, waiting for transfers between devices, on_device(): features = lax.all_gather(embedded, 'fsdp', axis=1, tiled=True)  109 us
    pad x24, local copies, waits for them, and re-layouts, modal_states(): return lax.associative_scan(pair_combine, (factors, inputs), axis=0)[1]  47.8 us
    ppermute x16, starting transfers between devices, from_behind(): return lax.ppermute(shard, axis, pairs)  41.6 us
    ppermute x16, waiting for transfers between devices, from_behind(): return lax.ppermute(shard, axis, pairs)  32.1 us
  transfers between devices with their start and end apart: 19, of which 19 were waited for; matrix products, arithmetic and copies ran while one was open for 1% of the time, Pallas kernels for 0%

commit v1 on v0

v1 whole, which is shorter than its diff:
```python
import functools

import jax
import jax.numpy as jnp
from jax import lax
from jax.experimental import pallas as pl
from jax.experimental.pallas import tpu as pltpu
from jax.sharding import PartitionSpec as P

MESH = pl.DeviceIdType.MESH
VMEM = pl.BlockSpec(memory_space=pltpu.VMEM)
ANY = pl.BlockSpec(memory_space=pl.ANY)
LIMIT = 60 * 1024 * 1024
NX, NY, NC = 4, 4, 8
CHUNKS = 8
LAG = 2
VOCAB = 512
MODES = 16
TAPS = 7


def place():
    f = lax.axis_index("fsdp")
    c = lax.axis_index("ctx")
    return f // 16, (f // 4) % 4, (f // 2) % 2, f % 2, c


def flat(x, y, h, k):
    return (x % 4) * 16 + (y % 4) * 4 + h * 2 + k


def greet(devices, count):
    barrier = pltpu.get_barrier_semaphore()
    for device, wanted in devices:
        if wanted is None:
            pl.semaphore_signal(barrier, inc=1, device_id=device, device_id_type=MESH)
        else:

            @pl.when(wanted)
            def _():
                pl.semaphore_signal(barrier, inc=1, device_id=device, device_id_type=MESH)

    pl.semaphore_wait(barrier, count)


def table_kernel(
    embed_ref, w_ref, tok_ref, cot_ref,
    p_ref, tokall_ref, cotall_ref,
    emb, acc, pre_in, suf_in, pre_out, suf_out, toks, cots,
    local_sem, a_send, a_recv, k_send, pre_send, pre_recv, suf_send, suf_recv,
    cot_send, cot_recv, tok_send, tok_recv,
):
    x, y, h, k, c = place()
    x0, y0 = c // 2, (c % 2) * 2
    dx, dy = (x - x0 + 4) % 4, (y - y0 + 4) % 4
    on_row = dy < 2
    source = jnp.logical_and(on_row, dx == 0)
    near = jnp.where(jnp.logical_or(dy == 0, dy == 3), 0, 1)
    own = near * 4 + h * 2 + k

    local = pltpu.make_async_copy(embed_ref, emb.at[own], local_sem)

    @pl.when(source)
    def _():
        local.start()

    me = flat(x, y, h, k)
    plane = [
        flat(x, y, 1 - h, k), flat(x + 1, y, h, k), flat(x + 3, y, h, k),
        flat(x, y + 1, h, k), flat(x, y + 3, h, k), flat(x, y, h, 1 - k),
    ]
    greet(
        [((d, c), None) for d in plane] + [((me, (c + o) % NC), None) for o in range(1, NC)],
        len(plane) + NC - 1,
    )

    def block_copy(slot, target, sem):
        return pltpu.make_async_remote_copy(
            src_ref=emb.at[slot], dst_ref=emb.at[slot], send_sem=sem, recv_sem=a_recv.at[slot],
            device_id=(target, c), device_id_type=MESH,
        )

    def arrived(slot):
        block_copy(slot, plane[0], a_send.at[0]).wait_recv()

    sends = []

    def send(slot, target, sem, when):
        copy = block_copy(slot, target, sem)
        sends.append((copy, when))
        if when is None:
            copy.start()
        else:

            @pl.when(when)
            def _():
                copy.start()

    @pl.when(source)
    def _():
        local.wait()

    send(own, plane[0], a_send.at[0], source)
    off_row = jnp.logical_not(on_row)
    extra = []
    for b in range(2):
        hb = h if b == 0 else 1 - h
        slot = near * 4 + hb * 2 + k
        if b == 0:

            @pl.when(jnp.logical_not(source))
            def _():
                arrived(slot)

        else:
            arrived(slot)
        base = 1 + b * 5
        send(slot, plane[1], a_send.at[base], jnp.logical_and(on_row, jnp.logical_or(dx == 0, dx == 1) if b == 0 else dx == 0))
        send(slot, plane[2], a_send.at[base + 1], jnp.logical_and(on_row, dx == 0 if b == 0 else jnp.logical_or(dx == 0, dx == 3)))
        send(slot, plane[3], a_send.at[base + 2], jnp.logical_or(on_row, dy == 2))
        send(slot, plane[4], a_send.at[base + 3], jnp.logical_or(on_row, dy == 3))
        send(slot, plane[5], k_send.at[b], None)
        if b == 0:
            for o in range(1, NC):
                target = (me, (c + o) % NC)
                cot_copy = pltpu.make_async_remote_copy(
                    src_ref=cot_ref, dst_ref=cots.at[c], send_sem=cot_send.at[o - 1], recv_sem=cot_recv.at[o - 1],
                    device_id=target, device_id_type=MESH,
                )
                tok_copy = pltpu.make_async_remote_copy(
                    src_ref=tok_ref, dst_ref=toks.at[c], send_sem=tok_send.at[o - 1], recv_sem=tok_recv.at[o - 1],
                    device_id=target, device_id_type=MESH,
                )
                cot_copy.start()
                tok_copy.start()
                extra += [cot_copy, tok_copy]
    for b in range(2):
        hb = h if b == 0 else 1 - h
        slot = (1 - near) * 4 + hb * 2 + k
        arrived(slot)
        send(slot, plane[5], k_send.at[2 + b], None)
    for q in range(4):
        arrived(q * 2 + 1 - k)

    total = None
    for q in range(4):
        left = jnp.concatenate([emb[2 * q], emb[2 * q + 1]], axis=1)
        right = jnp.concatenate([w_ref[g, pl.ds(q * 256, 256), :] for g in range(3)], axis=1)
        part = jnp.dot(left, right, preferred_element_type=jnp.float32)
        total = part if total is None else total + part
    acc[...] = total.reshape(acc.shape)

    rows = acc.shape[1]

    @pl.when(c == 0)
    def _():
        pre_in[...] = jnp.zeros_like(pre_in)

    @pl.when(c == NC - 1)
    def _():
        suf_in[...] = jnp.zeros_like(suf_in)

    def chain(i, inbox, outbox, send_sem, recv_sem, to):
        return pltpu.make_async_remote_copy(
            src_ref=outbox.at[i], dst_ref=inbox.at[i], send_sem=send_sem.at[i], recv_sem=recv_sem.at[i],
            device_id=(me, to), device_id_type=MESH,
        )

    up = (c + 1) % NC
    down = (c + NC - 1) % NC

    def turn(s, _):
        i = s - LAG * c

        @pl.when(jnp.logical_and(i >= 0, i < CHUNKS))
        def _():
            @pl.when(c > 0)
            def _():
                chain(i, pre_in, pre_out, pre_send, pre_recv, up).wait_recv()

            @pl.when(c < NC - 1)
            def _():
                pre_out[i] = acc[i] + pre_in[i]
                chain(i, pre_in, pre_out, pre_send, pre_recv, up).start()

        e = s - LAG * (NC - 1 - c)

        @pl.when(jnp.logical_and(e >= 0, e < CHUNKS))
        def _():
            @pl.when(c < NC - 1)
            def _():
                chain(e, suf_in, suf_out, suf_send, suf_recv, down).wait_recv()

            @pl.when(c > 0)
            def _():
                suf_out[e] = acc[e] + suf_in[e]
                chain(e, suf_in, suf_out, suf_send, suf_recv, down).start()

        return 0

    lax.fori_loop(0, LAG * (NC - 1) + CHUNKS, turn, 0)

    def finish(i, _):
        both = acc[i] + pre_in[i] + suf_in[i]
        p_ref[pl.ds(pl.multiple_of(i * rows, rows), rows), :] = both.astype(jnp.bfloat16)

        @pl.when(c < NC - 1)
        def _():
            chain(i, pre_in, pre_out, pre_send, pre_recv, up).wait_send()

        @pl.when(c > 0)
        def _():
            chain(i, suf_in, suf_out, suf_send, suf_recv, down).wait_send()

        return 0

    lax.fori_loop(0, CHUNKS, finish, 0)

    cots[c] = cot_ref[...]
    toks[c] = tok_ref[...]
    for copy in extra:
        copy.wait()
    for i in range(NC):
        cotall_ref[i] = cots[i]
        tokall_ref[pl.ds(i, 1), :] = toks[i]
    for copy, when in sends:
        if when is None:
            copy.wait_send()
        else:

            @pl.when(when)
            def _():
                copy.wait_send()


def shifted_up(value, by, row):
    return jnp.where(row >= by, pltpu.roll(value, by, 0), 0.0)


def shifted_down(value, by, row):
    return jnp.where(row < 8 - by, pltpu.roll(value, 8 - by, 0), 0.0)


def scan_modes(drive_at, out_ref, rates_ref, res_ref, backward):
    row = lax.broadcasted_iota(jnp.int32, (8, 128), 0)
    shifted = shifted_down if backward else shifted_up
    length = 128

    def spread(ref, m):
        return jnp.broadcast_to(ref[m : m + 1, :], (8, 128))

    def at(j):
        j = length - 1 - j if backward else j
        return pl.ds(pl.multiple_of(j * 8, 8), 8)

    decay = [jnp.exp(-spread(rates_ref, m)) for m in range(MODES)]

    def ends(j, state):
        drive = drive_at(at(j))
        return tuple(decay[m] * state[m] + drive for m in range(MODES))

    zero = jnp.zeros((8, 128), jnp.float32)
    state = lax.fori_loop(0, length, ends, (zero,) * MODES, unroll=4)
    entering = []
    for m in range(MODES):
        rate = spread(rates_ref, m)
        whole = state[m]
        for by in (1, 2, 4):
            whole = whole + jnp.exp(-rate * float(length * by)) * shifted(whole, by, row)
        entering.append(shifted(whole, 1, row))
    weight = [spread(res_ref, m) for m in range(MODES)]

    def outs(j, state):
        where = at(j)
        drive = drive_at(where)
        state = tuple(decay[m] * state[m] + drive for m in range(MODES))
        terms = [weight[m] * state[m] for m in range(MODES)]
        while len(terms) > 1:
            terms = [a + b for a, b in zip(terms[::2], terms[1::2])]
        out_ref[where, :] = terms[0]
        return state

    lax.fori_loop(0, length, outs, tuple(entering), unroll=4)


def mix_kernel(
    p_ref, tok_ref, cot_ref, taps_ref, rates_ref, res_ref, w_ref,
    mixed_ref, part_ref,
    z, filt, cot, drive, glong, lo, gd, gz, lhs,
):
    c = lax.axis_index("ctx")
    halo = 8
    row = lax.broadcasted_iota(jnp.int32, (8, 128), 0)
    lane = lax.broadcasted_iota(jnp.int32, (8, VOCAB), 1)

    for s in range(NC):
        cot[pl.ds(s, 128, stride=8), :] = cot_ref[s].astype(jnp.float32)

    def pick(i, toks):
        rows = []
        for j in range(0, 16, 2):
            two = [jnp.where(toks[:, j + e : j + e + 1] == lane, 1.0, 0.0) for e in range(2)]
            rows.append(jnp.concatenate(two, axis=0).astype(jnp.bfloat16))
        hot = jnp.concatenate(rows, axis=0)
        found = jnp.dot(hot, p_ref[...], preferred_element_type=jnp.float32)
        start = pl.ds(pl.multiple_of((halo + i * 16) * 8, 128 // 2), 128)
        for g in range(3):
            z[g, start, :] = found[:, g * 128 : (g + 1) * 128]
        return pltpu.roll(toks, 112, 1)

    lax.fori_loop(0, 8, pick, tok_ref[...])
    for g in range(3):
        for d in range(1, TAPS):
            z[g, pl.ds((halo - d) * 8, 8), :] = shifted_up(z[g, pl.ds((halo + 128 - d) * 8, 8), :], 1, row)

    def filter_rows(i, _):
        base = i * 64
        for g in range(3):
            value = None
            for d in range(TAPS):
                term = taps_ref[g, d : d + 1, :] * z[g, pl.ds(pl.multiple_of(base + (halo - d) * 8, 8), 64), :]
                value = term if value is None else value + term
            filt[g, pl.ds(pl.multiple_of(base, 64), 64), :] = value
        here = pl.ds(pl.multiple_of(base, 64), 64)
        drive[here, :] = filt[1, here, :] * filt[2, here, :]
        glong[here, :] = cot[here, :] * filt[0, here, :]
        return 0

    lax.fori_loop(0, 16, filter_rows, 0)
    scan_modes(lambda at: drive[at, :], lo, rates_ref, res_ref, False)
    scan_modes(lambda at: glong[at, :], gd, rates_ref, res_ref, True)

    def grads(i, _):
        here = pl.ds(pl.multiple_of(i * 64, 64), 64)
        long_out, grad_drive = lo[here, :], gd[here, :]
        z[0, here, :] = cot[here, :] * long_out
        z[1, here, :] = grad_drive * filt[2, here, :]
        z[2, here, :] = grad_drive * filt[1, here, :]
        lo[here, :] = filt[0, here, :] * long_out
        return 0

    lax.fori_loop(0, 16, grads, 0)
    mixed_ref[...] = lo[pl.ds(c, 128, stride=8), :].astype(jnp.bfloat16)
    for g in range(3):
        for d in range(TAPS - 1):
            z[g, pl.ds((128 + d) * 8, 8), :] = shifted_down(z[g, pl.ds(d * 8, 8), :], 1, row)

    def adjoint_rows(i, _):
        base = i * 64
        for g in range(3):
            value = None
            for d in range(TAPS):
                term = taps_ref[g, d : d + 1, :] * z[g, pl.ds(pl.multiple_of(base + d * 8, 8), 64), :]
                value = term if value is None else value + term
            gz[g, pl.ds(pl.multiple_of(base, 64), 64), :] = value
        return 0

    lax.fori_loop(0, 16, adjoint_rows, 0)
    for s in range(NC):
        for g in range(3):
            lhs[pl.ds(s * 128, 128), pl.ds(g * 128, 128)] = gz[g, pl.ds(s, 128, stride=8), :].astype(jnp.bfloat16)
    for n in range(4):
        yb, hh = n // 2, n % 2
        right = jnp.concatenate([w_ref[g, pl.ds(n * 256, 256), :] for g in range(3)], axis=1)
        out = lax.dot_general(
            lhs[...], right, (((1,), (1,)), ((), ())), preferred_element_type=jnp.float32
        ).astype(jnp.bfloat16)
        for s in range(NC):
            xo, yo = s // 2, yb * 2 + s % 2
            a, b = (xo, yo) if hh == 0 else (yo, xo)
            for kk in range(2):
                part_ref[kk, hh, a, b] = out[s * 128 : (s + 1) * 128, kk * 128 : (kk + 1) * 128]


def sum_kernel(
    part_ref, out_ref,
    core_in, first_out, first_in, second_out, second_in, last_out, last_in,
    core_send, core_recv, first_send, first_recv, second_send, second_recv, last_send, last_recv,
):
    x, y, h, k, c = place()
    x0, y0 = c // 2, (c % 2) * 2
    partner = (flat(x, y, h, 1 - k), c)
    xs = [(flat(x + o, y, h, k), c) for o in range(1, 4)]
    ys = [(flat(x, y + o, h, k), c) for o in range(1, 4)]
    owner = [(flat(x0, y0 + y // 2, e, k), 2 * x + y % 2) for e in range(2)]
    from_c = 2 * x + y // 2
    givers = [(flat(c // 2, (y % 2) * 2 + c % 2, e, k), from_c) for e in range(2)]
    loop = jnp.logical_and(jnp.logical_and(x == x0, y == y0 + y // 2), c == 2 * x + y % 2)
    foreign = [jnp.logical_not(jnp.logical_and(loop, h == e)) for e in range(2)]
    greet(
        [(d, None) for d in [partner] + xs + ys] + [(givers[e], foreign[e]) for e in range(2)],
        9 - loop.astype(jnp.int32),
    )

    def core_copy(e, a):
        return pltpu.make_async_remote_copy(
            src_ref=part_ref.at[1 - k, e, a], dst_ref=core_in.at[e, a],
            send_sem=core_send.at[e, a], recv_sem=core_recv.at[e, a], device_id=partner, device_id_type=MESH,
        )

    spots = [x, y]
    lines = [xs, ys]

    def first_copy(e, o):
        return pltpu.make_async_remote_copy(
            src_ref=first_out.at[e, o], dst_ref=first_in.at[e, o - 1],
            send_sem=first_send.at[e, o - 1], recv_sem=first_recv.at[e, o - 1],
            device_id=lines[e][o - 1], device_id_type=MESH,
        )

    def second_copy(e, o):
        return pltpu.make_async_remote_copy(
            src_ref=second_out.at[e, o], dst_ref=second_in.at[e, o - 1],
            send_sem=second_send.at[e, o - 1], recv_sem=second_recv.at[e, o - 1],
            device_id=lines[1 - e][o - 1], device_id_type=MESH,
        )

    def last_copy(e):
        return pltpu.make_async_remote_copy(
            src_ref=last_out.at[e], dst_ref=last_in.at[h],
            send_sem=last_send.at[e], recv_sem=last_recv.at[h], device_id=owner[e], device_id_type=MESH,
        )

    def last_wait(e):
        pltpu.make_async_remote_copy(
            src_ref=last_out.at[e], dst_ref=last_in.at[e],
            send_sem=last_send.at[e], recv_sem=last_recv.at[e], device_id=partner, device_id_type=MESH,
        ).wait_recv()

    order = [2, 1, 3, 0]
    for o in order:
        for e in range(2):
            core_copy(e, (spots[e] + o) % 4).start()
    for o in order:
        for e in range(2):
            a = (spots[e] + o) % 4
            core_copy(e, a).wait_recv()
            both = part_ref[k, e, a].astype(jnp.float32) + core_in[e, a].astype(jnp.float32)
            first_out[e, o] = both.astype(jnp.bfloat16)
            if o:
                first_copy(e, o).start()
    for e in range(2):
        for o in range(1, 4):
            first_copy(e, o).wait_recv()
    for o in order:
        for e in range(2):
            b = (spots[1 - e] + o) % 4
            both = first_out[e, 0, b].astype(jnp.float32)
            for i in range(3):
                both = both + first_in[e, i, b].astype(jnp.float32)
            second_out[e, o] = both.astype(jnp.bfloat16)
            if o:
                second_copy(e, o).start()
    for e in range(2):
        both = second_out[e, 0].astype(jnp.float32)
        for o in range(1, 4):
            second_copy(e, o).wait_recv()
            both = both + second_in[e, o - 1].astype(jnp.float32)
        last_out[e] = both.astype(jnp.bfloat16)

        @pl.when(foreign[e])
        def _():
            last_copy(e).start()

        @pl.when(jnp.logical_not(foreign[e]))
        def _():
            last_in[e] = last_out[e]

    for e in range(2):

        @pl.when(foreign[e])
        def _():
            last_wait(e)

    out_ref[...] = (last_in[0].astype(jnp.float32) + last_in[1].astype(jnp.float32)).astype(jnp.bfloat16)
    for e in range(2):
        for a in range(4):
            core_copy(e, (spots[e] + a) % 4).wait_send()
        for o in range(1, 4):
            first_copy(e, o).wait_send()
            second_copy(e, o).wait_send()

        @pl.when(foreign[e])
        def _():
            last_copy(e).wait_send()


def on_device(token_ids, embed, w_in, taps, rates, residues, cotangent):
    bf16, f32, i32 = jnp.bfloat16, jnp.float32, jnp.int32
    dma = pltpu.SemaphoreType.DMA
    w = w_in.transpose(1, 0, 2)
    taps = taps.transpose(1, 0, 2)
    rows = VOCAB // CHUNKS
    p, toks, cots = pl.pallas_call(
        table_kernel,
        out_shape=(
            jax.ShapeDtypeStruct((VOCAB, 384), bf16),
            jax.ShapeDtypeStruct((NC, 128), i32),
            jax.ShapeDtypeStruct((NC, 128, 128), bf16),
        ),
        in_specs=[ANY, VMEM, VMEM, VMEM],
        out_specs=(VMEM, VMEM, VMEM),
        scratch_shapes=[
            pltpu.VMEM((8, VOCAB, 128), bf16),
            pltpu.VMEM((CHUNKS, rows, 384), f32),
            pltpu.VMEM((CHUNKS, rows, 384), f32),
            pltpu.VMEM((CHUNKS, rows, 384), f32),
            pltpu.VMEM((CHUNKS, rows, 384), f32),
            pltpu.VMEM((CHUNKS, rows, 384), f32),
            pltpu.VMEM((NC, 1, 128), i32),
            pltpu.VMEM((NC, 128, 128), bf16),
            dma, dma((11,)), dma((8,)), dma((4,)),
            dma((CHUNKS,)), dma((CHUNKS,)), dma((CHUNKS,)), dma((CHUNKS,)),
            dma((NC - 1,)), dma((NC - 1,)), dma((NC - 1,)), dma((NC - 1,)),
        ],
        compiler_params=pltpu.CompilerParams(collective_id=0, has_side_effects=True, vmem_limit_bytes=LIMIT),
        name="table",
    )(embed, w, token_ids.reshape(1, 128), cotangent)
    wide = pltpu.VMEM((1024, 128), f32)
    mixed, part = pl.pallas_call(
        mix_kernel,
        out_shape=(
            jax.ShapeDtypeStruct((128, 128), bf16),
            jax.ShapeDtypeStruct((2, 2, 4, 4, 128, 128), bf16),
        ),
        in_specs=[VMEM] * 7,
        out_specs=(VMEM, VMEM),
        scratch_shapes=[
            pltpu.VMEM((3, 136 * 8, 128), f32), pltpu.VMEM((3, 1024, 128), f32),
            wide, wide, wide, wide, wide,
            pltpu.VMEM((3, 1024, 128), f32), pltpu.VMEM((1024, 384), bf16),
        ],
        compiler_params=pltpu.CompilerParams(vmem_limit_bytes=LIMIT),
        name="mix",
    )(p, toks, cots, taps, rates, residues, w)
    own = pl.pallas_call(
        sum_kernel,
        out_shape=jax.ShapeDtypeStruct((128, 128), bf16),
        in_specs=[VMEM],
        out_specs=VMEM,
        scratch_shapes=[
            pltpu.VMEM((2, 4, 4, 128, 128), bf16), pltpu.VMEM((2, 4, 4, 128, 128), bf16),
            pltpu.VMEM((2, 3, 4, 128, 128), bf16), pltpu.VMEM((2, 4, 128, 128), bf16),
            pltpu.VMEM((2, 3, 128, 128), bf16), pltpu.VMEM((2, 128, 128), bf16), pltpu.VMEM((2, 128, 128), bf16),
            dma((2, 4)), dma((2, 4)), dma((2, 3)), dma((2, 3)), dma((2, 3)), dma((2, 3)), dma((2,)), dma((2,)),
        ],
        compiler_params=pltpu.CompilerParams(collective_id=1, has_side_effects=True, vmem_limit_bytes=LIMIT),
        name="sums",
    )(part)
    return mixed, own


def solution(mesh):
    in_specs = (
        P("ctx"),
        P(None, "fsdp"),
        P("ctx", None, "fsdp"),
        P(None, None, "fsdp"),
        P(None, "fsdp"),
        P(None, "fsdp"),
        P("ctx", "fsdp"),
    )
    out_specs = (P("ctx", "fsdp"), P("ctx", "fsdp"))
    return jax.shard_map(on_device, mesh=mesh, in_specs=in_specs, out_specs=out_specs, check_vma=False)
```

time: 1030 us -> 131 us (0.13)
  waiting for transfers between devices: 878 us -> 0 us
  Pallas kernels: 0 us -> 127 us
  local copies, waits for them, and re-layouts: 58 us -> 1.38 us
  starting transfers between devices: 41.7 us -> 0 us
  matrix products: 14 us -> 0 us
  between operations: 14.5 us -> 0.65 us
  other arithmetic: 11.6 us -> 0 us
    reduce_scatter x1 -> x0, waiting for transfers between devices: 589 us -> none  [on_device(): lax.psum_scatter(lax.dot_general(whole_w, grad_rows, (((1,), (1,)), ((),...]
    all_gather x2 -> x0, waiting for transfers between devices: 256 us -> none  [the longest x1 146 us: on_device(): lax.all_gather(w_in, 'ctx', axis=0, tiled=True)]
    pallas_call x0 -> x3, Pallas kernels: none -> 127 us  [the longest x1 84.1 us: on_device(): pl.pallas_call(table_kernel, out_shape=(jax.ShapeDtypeStruct((VOCAB, 384)...]
    pad x24 -> x0, local copies, waits for them, and re-layouts: 47.8 us -> none  [modal_states(): return lax.associative_scan(pair_combine, (factors, inputs), axis=0)[1]]
    ppermute x16 -> x0, starting transfers between devices: 41.6 us -> none  [from_behind(): return lax.ppermute(shard, axis, pairs)]
    ppermute x16 -> x0, waiting for transfers between devices: 32.1 us -> none  [from_behind(): return lax.ppermute(shard, axis, pairs)]
    dot_general x3 -> x0, matrix products: 14 us -> none  [the longest x1 7.12 us: on_device(): lax.dot_general(whole_w, grad_rows, (((1,), (1,)), ((), ())), preferred_e...]
  transfers between devices with their start and end apart: 19 -> 0, of which waited for: 19 -> 0; matrix products, arithmetic and copies ran while one was open for 1% -> 0% of each run, Pallas kernels for 0% -> 0%
where the time goes in v1:
time: 131 us; the launch traced here: 129 us
  Pallas kernels  127 us (97%)
  local copies, waits for them, and re-layouts  1.38 us (1%)
    pallas_call x1, Pallas kernels, on_device(): pl.pallas_call(table_kernel, out_shape=(jax.ShapeDtypeStruct((VOCAB, 384)...  84.1 us
    pallas_call x1, Pallas kernels, on_device(): pl.pallas_call(sum_kernel, out_shape=jax.ShapeDtypeStruct((128, 128), bf1...  30.8 us
    pallas_call x1, Pallas kernels, on_device(): pl.pallas_call(mix_kernel, out_shape=(jax.ShapeDtypeStruct((128, 128), bf...  12.2 us

profile of v1, /device:TPU:1, one launch (start us, length us, event | category | flops | bytes accessed | tf_op | source)
XLA Modules:
  0.0 129.1 jit_solution(1568521836261712532)
XLA Ops:
  0.6 84.1 %table.1 = (bf16[512,384]{1,0:T(8,128)(2,1)}, s32[8,128]{1,0:T(8,128)}, bf16[8,128,128]{2,1,0:T(8,128)(2,1)}) custom-call(bf16[512,128]{1,0:T(8,128)(2,1)} %embed_ref.1, bf16[3,1024,128]{2,1,0:T(8,128)(2,1)} %bitcast.3, s32[1,128]{1,0:T(1,128)} %bitcast.6, bf16[128,128]{1,0:T(8,128)(2,1)} %cot_ref.1), custom_call_target="tpu_custom_call" | custom-call | tf_op jit(solution)/shard_map/table/pallas_call | solution.py:494
  84.7 12.2 %mix.1 = (bf16[128,128]{1,0:T(8,128)(2,1)}, bf16[2,2,4,4,128,128]{5,4,3,2,1,0:T(8,128)(2,1)}) custom-call(bf16[512,384]{1,0:T(8,128)(2,1)} %get-tuple-element.7.p_ref, s32[8,128]{1,0:T(8,128)} %get-tuple-element.8.tok_ref, bf16[8,128,128]{2,1,0:T(8,128)(2,1)} %get-tuple-element.9.cot_ref, f32[3,7,128]{2,1,0:T(8,128)} %bitcast.5, f32[16,128]{1,0:T(8,128)} %rates_ref.1, ...), custom_call_target="tpu_custom_call" | custom-call | tf_op jit(solution)/shard_map/mix/pallas_call | solution.py:520
  96.9 30.8 %sums.1 = bf16[128,128]{1,0:T(8,128)(2,1)} custom-call(bf16[2,2,4,4,128,128]{5,4,3,2,1,0:T(8,128)(2,1)} %get-tuple-element.11.part_ref), custom_call_target="tpu_custom_call" | custom-call | tf_op jit(solution)/shard_map/sums/pallas_call | solution.py:536
  127.7 1.4 %copy.10 = bf16[128,128]{1,0:T(8,128)(2,1)} copy(bf16[128,128]{1,0:T(8,128)(2,1)} %sums.1) | data formatting | bytes 65536

commit v2 on v1

v2 whole, which is shorter than its diff:
```python
import functools

import jax
import jax.numpy as jnp
from jax import lax
from jax.experimental import pallas as pl
from jax.experimental.pallas import tpu as pltpu
from jax.sharding import PartitionSpec as P

MESH = pl.DeviceIdType.MESH
VMEM = pl.BlockSpec(memory_space=pltpu.VMEM)
ANY = pl.BlockSpec(memory_space=pl.ANY)
LIMIT = 60 * 1024 * 1024
NC = 8
VOCAB = 512
MODES = 16
TAPS = 7


def place():
    f = lax.axis_index("fsdp")
    c = lax.axis_index("ctx")
    return f // 16, (f // 4) % 4, (f // 2) % 2, f % 2, c


def flat(x, y, h, k):
    return (x % 4) * 16 + (y % 4) * 4 + h * 2 + k


def greet(devices, count):
    barrier = pltpu.get_barrier_semaphore()
    for device, wanted in devices:
        if wanted is None:
            pl.semaphore_signal(barrier, inc=1, device_id=device, device_id_type=MESH)
        else:

            @pl.when(wanted)
            def _():
                pl.semaphore_signal(barrier, inc=1, device_id=device, device_id_type=MESH)

    pl.semaphore_wait(barrier, count)


def table_kernel(
    embed_ref, w_ref, tok_ref, cot_ref,
    p_ref, tokall_ref, cotall_ref,
    emb, acc, part_out, part_in, pair_out, pair_in, table, toks, cots,
    local_sem, half_send, x_send, y_send, k_send, a_recv,
    part_send, part_recv, pair_send, pair_recv, done_send, done_recv,
    cot_send, cot_recv, tok_send, tok_recv,
):
    f32, bf16 = jnp.float32, jnp.bfloat16
    x, y, h, k, c = place()
    me = flat(x, y, h, k)
    mine = 2 * x + y // 2
    yb = y % 2
    edge = jnp.where(mine < NC // 2, NC - 1, 0)
    x0, y0 = c // 2, (c % 2) * 2
    dy = (y - y0 + 4) % 4
    on_row = dy < 2
    source = mine == c
    near = jnp.where(dy == 1, 1, 0)
    own = yb * 4 + h * 2 + k

    xs = [flat(x + o, y, h, k) for o in range(1, 4)]
    ys = [flat(x, y + o, h, k) for o in range(1, 4)]
    partner = flat(x, y, h, 1 - k)
    other = flat(x, y, 1 - h, k)
    gives = c == edge
    greet(
        [((d, c), None) for d in xs + ys + [partner]]
        + [((me, (c + o) % NC), None) for o in range(1, NC)]
        + [((other, edge), source)],
        7 + NC - 1 + gives.astype(jnp.int32),
    )

    local = pltpu.make_async_copy(embed_ref, emb.at[own], local_sem)

    def block_copy(slot, target, sem, src=None, to=c):
        return pltpu.make_async_remote_copy(
            src_ref=emb.at[slot] if src is None else src, dst_ref=emb.at[slot], send_sem=sem,
            recv_sem=a_recv.at[slot], device_id=(target, to), device_id_type=MESH,
        )

    def arrived(slot):
        block_copy(slot, partner, k_send.at[0]).wait_recv()

    sends = []

    def send(copy, when):
        sends.append((copy, when))
        if when is None:
            copy.start()
        else:

            @pl.when(when)
            def _():
                copy.start()

    send(block_copy(own, other, half_send, embed_ref, mine), gives)

    @pl.when(source)
    def _():
        local.start()

    for o in (2, 1, 3):
        send(block_copy(own, xs[o - 1], x_send.at[0, o - 1], embed_ref), source)

    @pl.when(source)
    def _():
        local.wait()

    def slot_of(row, b):
        return row * 4 + (h if b == 0 else 1 - h) * 2 + k

    extra = []
    for b in range(2):
        slot = slot_of(near, b)
        if b == 0:

            @pl.when(jnp.logical_not(source))
            def _():
                arrived(slot)

        else:
            arrived(slot)
            for o in (2, 1, 3):
                send(block_copy(slot, xs[o - 1], x_send.at[1, o - 1]), source)
        for o in (2, 1, 3):
            send(block_copy(slot, ys[o - 1], y_send.at[b, o - 1]), on_row)
        send(block_copy(slot, partner, k_send.at[b]), None)
        if b == 0:
            for o in range(1, NC):
                target = (me, (c + o) % NC)
                for src, dst, ss, rs in (
                    (cot_ref, cots, cot_send, cot_recv), (tok_ref, toks, tok_send, tok_recv)
                ):
                    copy = pltpu.make_async_remote_copy(
                        src_ref=src, dst_ref=dst.at[c], send_sem=ss.at[o - 1], recv_sem=rs.at[o - 1],
                        device_id=target, device_id_type=MESH,
                    )
                    copy.start()
                    extra.append(copy)
            far = slot_of(1 - near, 0)
            arrived(far)
            send(block_copy(far, partner, k_send.at[2]), None)

    def lane(e, b):
        return e * 4 + (h if b == 0 else 1 - h) * 2

    def product(rows, b):
        total = None
        for e in range(2):
            j = lane(e, b)
            left = jnp.concatenate([emb[j, rows, :], emb[j + 1, rows, :]], axis=1)
            at = pl.ds(pl.multiple_of(j * 128, 256), 256)
            right = jnp.concatenate([w_ref[g, at, :] for g in range(3)], axis=1)
            part = jnp.dot(left, right, preferred_element_type=f32)
            total = part if total is None else total + part
        return total

    for e in range(2):
        arrived(lane(e, 0) + 1 - k)
    for q in range(4):
        rows = pl.ds(q * 128, 128)
        acc[q] = product(rows, 0)
    far = slot_of(1 - near, 1)
    arrived(far)
    send(block_copy(far, partner, k_send.at[3]), None)
    for e in range(2):
        arrived(lane(e, 1) + 1 - k)

    q = c % 4
    base = c - q

    def part_copy(o, s):
        return pltpu.make_async_remote_copy(
            src_ref=part_out.at[o - 1, s], dst_ref=part_in.at[o - 1, s], send_sem=part_send.at[o - 1, s],
            recv_sem=part_recv.at[o - 1, s], device_id=(me, base + (q + o) % 4), device_id_type=MESH,
        )

    def pair_copy(s):
        return pltpu.make_async_remote_copy(
            src_ref=pair_out.at[s], dst_ref=pair_in.at[s], send_sem=pair_send.at[s], recv_sem=pair_recv.at[s],
            device_id=(me, (c + 4) % NC), device_id_type=MESH,
        )

    def done_copy(o, s):
        return pltpu.make_async_remote_copy(
            src_ref=table.at[q, s], dst_ref=table.at[q, s], send_sem=done_send.at[o - 1, s],
            recv_sem=done_recv.at[o - 1, s], device_id=(me, base + (q + o) % 4), device_id_type=MESH,
        )

    for s in range(2):
        for o in (3, 1, 2, 0):
            group = (q + o) % 4
            rows = pl.ds(pl.multiple_of(group * 128 + s * 64, 64), 64)
            half = pl.ds(s * 64, 64)
            total = acc[group, half, :] + product(rows, 1)
            if o:
                part_out[o - 1, s] = total.astype(bf16)
                part_copy(o, s).start()
            else:
                acc[group, half, :] = total
    for s in range(2):
        half = pl.ds(s * 64, 64)
        total = acc[q, half, :]
        for o in range(1, 4):
            part_copy(o, s).wait_recv()
            total = total + part_in[o - 1, s].astype(f32)
        acc[q, half, :] = total
        pair_out[s] = total.astype(bf16)
        pair_copy(s).start()
    for s in range(2):
        half = pl.ds(s * 64, 64)
        pair_copy(s).wait_recv()
        table[q, s] = (acc[q, half, :] + pair_in[s].astype(f32)).astype(bf16)
        for o in (3, 1, 2):
            done_copy(o, s).start()

    cots[c] = cot_ref[...]
    toks[c] = tok_ref[...]
    for copy in extra:
        copy.wait()
    for i in range(NC):
        cotall_ref[i] = cots[i]
        tokall_ref[pl.ds(i, 1), :] = toks[i]
    for copy, when in sends:
        if when is None:
            copy.wait_send()
        else:

            @pl.when(when)
            def _():
                copy.wait_send()

    for s in range(2):
        pair_copy(s).wait_send()
        for o in range(1, 4):
            part_copy(o, s).wait_send()
            done_copy(o, s).wait()
    for i in range(4):
        for s in range(2):
            p_ref[pl.ds(i * 128 + s * 64, 64), :] = table[i, s]


def shifted_up(value, by, row):
    return jnp.where(row >= by, pltpu.roll(value, by, 0), 0.0)


def shifted_down(value, by, row):
    return jnp.where(row < 8 - by, pltpu.roll(value, 8 - by, 0), 0.0)


def scan_modes(drive_at, out_ref, rates_ref, res_ref, backward):
    row = lax.broadcasted_iota(jnp.int32, (8, 128), 0)
    shifted = shifted_down if backward else shifted_up
    length = 128

    def spread(ref, m):
        return jnp.broadcast_to(ref[m : m + 1, :], (8, 128))

    def at(j):
        j = length - 1 - j if backward else j
        return pl.ds(pl.multiple_of(j * 8, 8), 8)

    decay = [jnp.exp(-spread(rates_ref, m)) for m in range(MODES)]

    def ends(j, state):
        drive = drive_at(at(j))
        return tuple(decay[m] * state[m] + drive for m in range(MODES))

    zero = jnp.zeros((8, 128), jnp.float32)
    state = lax.fori_loop(0, length, ends, (zero,) * MODES, unroll=4)
    entering = []
    for m in range(MODES):
        rate = spread(rates_ref, m)
        whole = state[m]
        for by in (1, 2, 4):
            whole = whole + jnp.exp(-rate * float(length * by)) * shifted(whole, by, row)
        entering.append(shifted(whole, 1, row))
    weight = [spread(res_ref, m) for m in range(MODES)]

    def outs(j, state):
        where = at(j)
        drive = drive_at(where)
        state = tuple(decay[m] * state[m] + drive for m in range(MODES))
        terms = [weight[m] * state[m] for m in range(MODES)]
        while len(terms) > 1:
            terms = [a + b for a, b in zip(terms[::2], terms[1::2])]
        out_ref[where, :] = terms[0]
        return state

    lax.fori_loop(0, length, outs, tuple(entering), unroll=4)


def mix_kernel(
    p_ref, tok_ref, cot_ref, taps_ref, rates_ref, res_ref,
    mixed_ref, lhs_ref,
    z, filt, cot, drive, glong, lo, gd, gz,
):
    c = lax.axis_index("ctx")
    halo = 8
    row = lax.broadcasted_iota(jnp.int32, (8, 128), 0)
    lane = lax.broadcasted_iota(jnp.int32, (8, VOCAB), 1)

    for s in range(NC):
        cot[pl.ds(s, 128, stride=8), :] = cot_ref[s].astype(jnp.float32)

    def pick(i, toks):
        rows = []
        for j in range(0, 16, 2):
            two = [jnp.where(toks[:, j + e : j + e + 1] == lane, 1.0, 0.0) for e in range(2)]
            rows.append(jnp.concatenate(two, axis=0).astype(jnp.bfloat16))
        hot = jnp.concatenate(rows, axis=0)
        found = jnp.dot(hot, p_ref[...], preferred_element_type=jnp.float32)
        start = pl.ds(pl.multiple_of((halo + i * 16) * 8, 128 // 2), 128)
        for g in range(3):
            z[g, start, :] = found[:, g * 128 : (g + 1) * 128]
        return pltpu.roll(toks, 112, 1)

    lax.fori_loop(0, 8, pick, tok_ref[...])
    for g in range(3):
        for d in range(1, TAPS):
            z[g, pl.ds((halo - d) * 8, 8), :] = shifted_up(z[g, pl.ds((halo + 128 - d) * 8, 8), :], 1, row)

    def filter_rows(i, _):
        base = i * 64
        for g in range(3):
            value = None
            for d in range(TAPS):
                term = taps_ref[g, d : d + 1, :] * z[g, pl.ds(pl.multiple_of(base + (halo - d) * 8, 8), 64), :]
                value = term if value is None else value + term
            filt[g, pl.ds(pl.multiple_of(base, 64), 64), :] = value
        here = pl.ds(pl.multiple_of(base, 64), 64)
        drive[here, :] = filt[1, here, :] * filt[2, here, :]
        glong[here, :] = cot[here, :] * filt[0, here, :]
        return 0

    lax.fori_loop(0, 16, filter_rows, 0)
    scan_modes(lambda at: drive[at, :], lo, rates_ref, res_ref, False)
    scan_modes(lambda at: glong[at, :], gd, rates_ref, res_ref, True)

    def grads(i, _):
        here = pl.ds(pl.multiple_of(i * 64, 64), 64)
        long_out, grad_drive = lo[here, :], gd[here, :]
        z[0, here, :] = cot[here, :] * long_out
        z[1, here, :] = grad_drive * filt[2, here, :]
        z[2, here, :] = grad_drive * filt[1, here, :]
        lo[here, :] = filt[0, here, :] * long_out
        return 0

    lax.fori_loop(0, 16, grads, 0)
    mixed_ref[...] = lo[pl.ds(c, 128, stride=8), :].astype(jnp.bfloat16)
    for g in range(3):
        for d in range(TAPS - 1):
            z[g, pl.ds((128 + d) * 8, 8), :] = shifted_down(z[g, pl.ds(d * 8, 8), :], 1, row)

    def adjoint_rows(i, _):
        base = i * 64
        for g in range(3):
            value = None
            for d in range(TAPS):
                term = taps_ref[g, d : d + 1, :] * z[g, pl.ds(pl.multiple_of(base + d * 8, 8), 64), :]
                value = term if value is None else value + term
            gz[g, pl.ds(pl.multiple_of(base, 64), 64), :] = value
        return 0

    lax.fori_loop(0, 16, adjoint_rows, 0)
    for s in range(NC):
        start = (c + s) % NC
        for g in range(3):
            lhs_ref[pl.ds(s * 128, 128), pl.ds(g * 128, 128)] = gz[g, pl.ds(start, 128, stride=8), :].astype(jnp.bfloat16)


SPOT = {0: (0, 0), 1: (1, 0), 2: (0, 1), 3: (1, 1), 4: (2, 1), 5: (3, 1), 6: (2, 0), 7: (3, 0)}


def sum_kernel(
    lhs_ref, w_ref, out_ref,
    own, core_out, core_in, first_out, first_in, second_own, second_out, second_in, last_out, last_in,
    core_send, core_recv, first_send, first_recv, second_send, second_recv, last_send, last_recv,
):
    f32, bf16 = jnp.float32, jnp.bfloat16
    x, y, h, k, c = place()
    x0, y0 = c // 2, (c % 2) * 2
    dx, dy = (x - x0 + 4) % 4, (y - y0 + 4) % 4
    partner = (flat(x, y, h, 1 - k), c)
    xs = [(flat(x + o, y, h, k), c) for o in range(1, 4)]
    ys = [(flat(x, y + o, h, k), c) for o in range(1, 4)]
    yb = jnp.where(jnp.logical_or(dy == 1, dy == 2), 1, 0)
    far = jnp.where(dy >= 2, 1, 0)
    step = jnp.where(dx < 2, dx + 2 * far, dx + 4 - 2 * far)
    owner = [(flat(x0, y0 + yb, e, k), (c + step) % NC) for e in range(2)]
    from_c = 2 * x + y // 2
    back = (c - from_c + NC) % NC
    back_x = jnp.where(back < 4, back % 2, 2 + back % 2)
    back_far = jnp.where(back < 4, back // 2, 3 - back // 2)
    back_y = jnp.where(y % 2 == 0, 3 * back_far, 1 + back_far)
    givers = [(flat(x + back_x, (y // 2) * 2 + back_y, e, k), from_c) for e in range(2)]
    loop = jnp.logical_and(dx == 0, dy < 2)
    foreign = [jnp.logical_not(jnp.logical_and(loop, h == e)) for e in range(2)]
    greet(
        [(d, None) for d in [partner] + xs + ys] + [(givers[e], foreign[e]) for e in range(2)],
        9 - loop.astype(jnp.int32),
    )

    def core_copy(e, a):
        return pltpu.make_async_remote_copy(
            src_ref=core_out.at[e, a], dst_ref=core_in.at[e, a],
            send_sem=core_send.at[e, a], recv_sem=core_recv.at[e, a], device_id=partner, device_id_type=MESH,
        )

    spots = [dx, dy]
    lines = [xs, ys]

    def first_copy(e, o):
        return pltpu.make_async_remote_copy(
            src_ref=first_out.at[e, o - 1], dst_ref=first_in.at[e, o - 1],
            send_sem=first_send.at[e, o - 1], recv_sem=first_recv.at[e, o - 1],
            device_id=lines[e][o - 1], device_id_type=MESH,
        )

    def second_copy(e, o):
        return pltpu.make_async_remote_copy(
            src_ref=second_out.at[e, o - 1], dst_ref=second_in.at[e, o - 1],
            send_sem=second_send.at[e, o - 1], recv_sem=second_recv.at[e, o - 1],
            device_id=lines[1 - e][o - 1], device_id_type=MESH,
        )

    def last_copy(e):
        return pltpu.make_async_remote_copy(
            src_ref=last_out.at[e], dst_ref=last_in.at[h],
            send_sem=last_send.at[e], recv_sem=last_recv.at[h], device_id=owner[e], device_id_type=MESH,
        )

    def last_wait(e):
        pltpu.make_async_remote_copy(
            src_ref=last_out.at[e], dst_ref=last_in.at[e],
            send_sem=last_send.at[e], recv_sem=last_recv.at[e], device_id=partner, device_id_type=MESH,
        ).wait_recv()

    def tile(e, kk, store):
        starts = [pl.multiple_of(r * 512 + e * 256 + kk * 128, 128) for r in range(2)]
        right = jnp.concatenate(
            [jnp.concatenate([w_ref[g, pl.ds(at, 128), :] for g in range(3)], axis=1) for at in starts], axis=0
        )
        out = lax.dot_general(lhs_ref[...], right, (((1,), (1,)), ((), ())), preferred_element_type=f32)
        for s in range(NC):
            sx, sfar = SPOT[s]
            for r in range(2):
                sy = 3 * sfar if r == 0 else 1 + sfar
                a, b = (sx, sy) if e == 0 else (sy, sx)
                store(e, a, b, out[s * 128 : (s + 1) * 128, r * 128 : (r + 1) * 128])

    def to_core(e, a, b, value):
        core_out[e, a, b] = value.astype(bf16)

    def to_own(e, a, b, value):
        own[e, a, b] = value

    for e in range(2):
        tile(e, 1 - k, to_core)
        for a in range(4):
            core_copy(e, a).start()
    for e in range(2):
        tile(e, k, to_own)
    order = [2, 1, 3, 0]
    for o in order:
        for e in range(2):
            a = (spots[e] + o) % 4
            core_copy(e, a).wait_recv()
            both = own[e, a] + core_in[e, a].astype(f32)
            if o:
                first_out[e, o - 1] = both.astype(bf16)
                first_copy(e, o).start()
            else:
                own[e, a] = both
    for e in range(2):
        for o in range(1, 4):
            first_copy(e, o).wait_recv()
    for o in order:
        for e in range(2):
            b = (spots[1 - e] + o) % 4
            both = own[e, spots[e], b]
            for i in range(3):
                both = both + first_in[e, i, b].astype(f32)
            if o:
                second_out[e, o - 1] = both.astype(bf16)
                second_copy(e, o).start()
            else:
                second_own[e] = both
    for e in range(2):
        both = second_own[e]
        for o in range(1, 4):
            second_copy(e, o).wait_recv()
            both = both + second_in[e, o - 1].astype(f32)
        last_out[e] = both.astype(bf16)

        @pl.when(foreign[e])
        def _():
            last_copy(e).start()

        @pl.when(jnp.logical_not(foreign[e]))
        def _():
            last_in[e] = last_out[e]

    for e in range(2):

        @pl.when(foreign[e])
        def _():
            last_wait(e)

    out_ref[...] = (last_in[0].astype(f32) + last_in[1].astype(f32)).astype(bf16)
    for e in range(2):
        for a in range(4):
            core_copy(e, a).wait_send()
        for o in range(1, 4):
            first_copy(e, o).wait_send()
            second_copy(e, o).wait_send()

        @pl.when(foreign[e])
        def _():
            last_copy(e).wait_send()


def on_device(token_ids, embed, w_in, taps, rates, residues, cotangent):
    bf16, f32, i32 = jnp.bfloat16, jnp.float32, jnp.int32
    dma = pltpu.SemaphoreType.DMA
    w = w_in.transpose(1, 0, 2)
    taps = taps.transpose(1, 0, 2)
    p, toks, cots = pl.pallas_call(
        table_kernel,
        out_shape=(
            jax.ShapeDtypeStruct((VOCAB, 384), bf16),
            jax.ShapeDtypeStruct((NC, 128), i32),
            jax.ShapeDtypeStruct((NC, 128, 128), bf16),
        ),
        in_specs=[ANY, VMEM, VMEM, VMEM],
        out_specs=(VMEM, VMEM, VMEM),
        scratch_shapes=[
            pltpu.VMEM((8, VOCAB, 128), bf16),
            pltpu.VMEM((4, 128, 384), f32),
            pltpu.VMEM((3, 2, 64, 384), bf16), pltpu.VMEM((3, 2, 64, 384), bf16),
            pltpu.VMEM((2, 64, 384), bf16), pltpu.VMEM((2, 64, 384), bf16),
            pltpu.VMEM((4, 2, 64, 384), bf16),
            pltpu.VMEM((NC, 1, 128), i32),
            pltpu.VMEM((NC, 128, 128), bf16),
            dma, dma, dma((2, 3)), dma((2, 3)), dma((4,)), dma((8,)),
            dma((3, 2)), dma((3, 2)), dma((2,)), dma((2,)), dma((3, 2)), dma((3, 2)),
            dma((NC - 1,)), dma((NC - 1,)), dma((NC - 1,)), dma((NC - 1,)),
        ],
        compiler_params=pltpu.CompilerParams(collective_id=0, has_side_effects=True, vmem_limit_bytes=LIMIT),
        name="table",
    )(embed, w, token_ids.reshape(1, 128), cotangent)
    wide = pltpu.VMEM((1024, 128), f32)
    mixed, lhs = pl.pallas_call(
        mix_kernel,
        out_shape=(
            jax.ShapeDtypeStruct((128, 128), bf16),
            jax.ShapeDtypeStruct((1024, 384), bf16),
        ),
        in_specs=[VMEM] * 6,
        out_specs=(VMEM, VMEM),
        scratch_shapes=[
            pltpu.VMEM((3, 136 * 8, 128), f32), pltpu.VMEM((3, 1024, 128), f32),
            wide, wide, wide, wide, wide,
            pltpu.VMEM((3, 1024, 128), f32),
        ],
        compiler_params=pltpu.CompilerParams(vmem_limit_bytes=LIMIT),
        name="mix",
    )(p, toks, cots, taps, rates, residues)
    own = pl.pallas_call(
        sum_kernel,
        out_shape=jax.ShapeDtypeStruct((128, 128), bf16),
        in_specs=[VMEM, VMEM],
        out_specs=VMEM,
        scratch_shapes=[
            pltpu.VMEM((2, 4, 4, 128, 128), f32),
            pltpu.VMEM((2, 4, 4, 128, 128), bf16), pltpu.VMEM((2, 4, 4, 128, 128), bf16),
            pltpu.VMEM((2, 3, 4, 128, 128), bf16), pltpu.VMEM((2, 3, 4, 128, 128), bf16),
            pltpu.VMEM((2, 128, 128), f32),
            pltpu.VMEM((2, 3, 128, 128), bf16), pltpu.VMEM((2, 3, 128, 128), bf16),
            pltpu.VMEM((2, 128, 128), bf16), pltpu.VMEM((2, 128, 128), bf16),
            dma((2, 4)), dma((2, 4)), dma((2, 3)), dma((2, 3)), dma((2, 3)), dma((2, 3)), dma((2,)), dma((2,)),
        ],
        compiler_params=pltpu.CompilerParams(collective_id=1, has_side_effects=True, vmem_limit_bytes=LIMIT),
        name="sums",
    )(lhs, w)
    return mixed, own


def solution(mesh):
    in_specs = (
        P("ctx"),
        P(None, "fsdp"),
        P("ctx", None, "fsdp"),
        P(None, None, "fsdp"),
        P(None, "fsdp"),
        P(None, "fsdp"),
        P("ctx", "fsdp"),
    )
    out_specs = (P("ctx", "fsdp"), P("ctx", "fsdp"))
    return jax.shard_map(on_device, mesh=mesh, in_specs=in_specs, out_specs=out_specs, check_vma=False)
```

time: 131 us -> 109 us (0.83)
  the two profiles are of different devices: /device:TPU:1 before, /device:TPU:5 now
where the time goes in v2:
time: 109 us
  Pallas kernels  107 us (98%)
  local copies, waits for them, and re-layouts  1.38 us (1%)
    pallas_call x1, Pallas kernels, on_device(): pl.pallas_call(table_kernel, out_shape=(jax.ShapeDtypeStruct((VOCAB, 384)...  62.8 us
    pallas_call x1, Pallas kernels, on_device(): pl.pallas_call(sum_kernel, out_shape=jax.ShapeDtypeStruct((128, 128), bf1...  33.4 us
    pallas_call x1, Pallas kernels, on_device(): pl.pallas_call(mix_kernel, out_shape=(jax.ShapeDtypeStruct((128, 128), bf...  10.5 us

profile of v2, /device:TPU:5, one launch (start us, length us, event | category | flops | bytes accessed | tf_op | source)
XLA Modules:
  0.0 108.8 jit_solution(11852802450877513484)
XLA Ops:
  0.6 62.8 %table.1 = (bf16[512,384]{1,0:T(8,128)(2,1)}, s32[8,128]{1,0:T(8,128)}, bf16[8,128,128]{2,1,0:T(8,128)(2,1)}) custom-call(bf16[512,128]{1,0:T(8,128)(2,1)} %embed_ref.1, bf16[3,1024,128]{2,1,0:T(8,128)(2,1)} %bitcast.3, s32[1,128]{1,0:T(1,128)} %bitcast.6, bf16[128,128]{1,0:T(8,128)(2,1)} %cot_ref.1), custom_call_target="tpu_custom_call" | custom-call | tf_op jit(solution)/shard_map/table/pallas_call | solution.py:532
  63.5 10.5 %mix.1 = (bf16[128,128]{1,0:T(8,128)(2,1)}, bf16[1024,384]{1,0:T(8,128)(2,1)}) custom-call(bf16[512,384]{1,0:T(8,128)(2,1)} %get-tuple-element.7.p_ref, s32[8,128]{1,0:T(8,128)} %get-tuple-element.8.tok_ref, bf16[8,128,128]{2,1,0:T(8,128)(2,1)} %get-tuple-element.9.cot_ref, f32[3,7,128]{2,1,0:T(8,128)} %bitcast.5, f32[16,128]{1,0:T(8,128)} %rates_ref.1, ...), custom_call_target="tpu_custom_call" | custom-call | tf_op jit(solution)/shard_map/mix/pallas_call | solution.py:557
  74.0 33.4 %sums.1 = bf16[128,128]{1,0:T(8,128)(2,1)} custom-call(bf16[1024,384]{1,0:T(8,128)(2,1)} %get-tuple-element.11.lhs_ref, bf16[3,1024,128]{2,1,0:T(8,128)(2,1)} %bitcast.4), custom_call_target="tpu_custom_call" | custom-call | tf_op jit(solution)/shard_map/sums/pallas_call | solution.py:573
  107.4 1.4 %copy.10 = bf16[128,128]{1,0:T(8,128)(2,1)} copy(bf16[128,128]{1,0:T(8,128)(2,1)} %sums.1) | data formatting | bytes 65536

commit v3 on v2

--- a/solution.py
+++ b/solution.py
@@ -12,6 +12,8 @@
 ANY = pl.BlockSpec(memory_space=pl.ANY)
 LIMIT = 60 * 1024 * 1024
 NC = 8
+PIECES = 2
+PIECE = 256
 VOCAB = 512
 MODES = 16
 TAPS = 7
@@ -27,7 +29,7 @@
     return (x % 4) * 16 + (y % 4) * 4 + h * 2 + k
 
 
-def greet(devices, count):
+def hail(devices):
     barrier = pltpu.get_barrier_semaphore()
     for device, wanted in devices:
         if wanted is None:
@@ -38,7 +40,10 @@
             def _():
                 pl.semaphore_signal(barrier, inc=1, device_id=device, device_id_type=MESH)
 
-    pl.semaphore_wait(barrier, count)
+
+def greet(devices, count):
+    hail(devices)
+    pl.semaphore_wait(pltpu.get_barrier_semaphore(), count)
 
 
 def table_kernel(
@@ -67,23 +72,28 @@
     partner = flat(x, y, h, 1 - k)
     other = flat(x, y, 1 - h, k)
     gives = c == edge
+    q = c % 4
+    base = c - q
+    across = (c + 4) % NC
+    group = [(me, base + (q + o) % 4) for o in range(1, 4)]
     greet(
         [((d, c), None) for d in xs + ys + [partner]]
-        + [((me, (c + o) % NC), None) for o in range(1, NC)]
+        + [(d, None) for d in group + [(me, across)]]
         + [((other, edge), source)],
-        7 + NC - 1 + gives.astype(jnp.int32),
+        11 + gives.astype(jnp.int32),
     )
 
     local = pltpu.make_async_copy(embed_ref, emb.at[own], local_sem)
 
-    def block_copy(slot, target, sem, src=None, to=c):
-        return pltpu.make_async_remote_copy(
-            src_ref=emb.at[slot] if src is None else src, dst_ref=emb.at[slot], send_sem=sem,
-            recv_sem=a_recv.at[slot], device_id=(target, to), device_id_type=MESH,
-        )
-
-    def arrived(slot):
-        block_copy(slot, partner, k_send.at[0]).wait_recv()
+    def block_copy(slot, p, target, sem, src=None, to=c):
+        rows = pl.ds(p * PIECE, PIECE)
+        return pltpu.make_async_remote_copy(
+            src_ref=emb.at[slot, rows] if src is None else src.at[rows], dst_ref=emb.at[slot, rows], send_sem=sem,
+            recv_sem=a_recv.at[slot, p], device_id=(target, to), device_id_type=MESH,
+        )
+
+    def arrived(slot, p):
+        block_copy(slot, p, partner, k_send.at[0, 0]).wait_recv()
 
     sends = []
 
@@ -97,81 +107,90 @@
             def _():
                 copy.start()
 
-    send(block_copy(own, other, half_send, embed_ref, mine), gives)
+    for p in range(PIECES):
+        send(block_copy(own, p, other, half_send.at[p], embed_ref, mine), gives)
+    for p in range(PIECES):
+        for o in (2, 1, 3):
+            send(block_copy(own, p, xs[o - 1], x_send.at[0, o - 1, p], embed_ref), source)
 
     @pl.when(source)
     def _():
         local.start()
-
-    for o in (2, 1, 3):
-        send(block_copy(own, xs[o - 1], x_send.at[0, o - 1], embed_ref), source)
-
-    @pl.when(source)
-    def _():
         local.wait()
 
     def slot_of(row, b):
         return row * 4 + (h if b == 0 else 1 - h) * 2 + k
 
     extra = []
+
+    def spread(index, target, sem):
+        for src, dst, ss, rs in ((cot_ref, cots, cot_send, cot_recv), (tok_ref, toks, tok_send, tok_recv)):
+            copy = pltpu.make_async_remote_copy(
+                src_ref=src if sem < 4 else dst.at[index], dst_ref=dst.at[index], send_sem=ss.at[sem],
+                recv_sem=rs.at[sem], device_id=target, device_id_type=MESH,
+            )
+            copy.start()
+            extra.append(copy)
+
     for b in range(2):
         slot = slot_of(near, b)
+        for p in range(PIECES):
+            if b == 0:
+
+                @pl.when(jnp.logical_not(source))
+                def _():
+                    arrived(slot, p)
+
+            else:
+                arrived(slot, p)
+                for o in (2, 1, 3):
+                    send(block_copy(slot, p, xs[o - 1], x_send.at[1, o - 1, p]), source)
+            for o in (2, 1, 3):
+                send(block_copy(slot, p, ys[o - 1], y_send.at[b, o - 1, p]), on_row)
+            send(block_copy(slot, p, partner, k_send.at[b, p]), None)
         if b == 0:
-
-            @pl.when(jnp.logical_not(source))
-            def _():
-                arrived(slot)
-
-        else:
-            arrived(slot)
-            for o in (2, 1, 3):
-                send(block_copy(slot, xs[o - 1], x_send.at[1, o - 1]), source)
-        for o in (2, 1, 3):
-            send(block_copy(slot, ys[o - 1], y_send.at[b, o - 1]), on_row)
-        send(block_copy(slot, partner, k_send.at[b]), None)
-        if b == 0:
-            for o in range(1, NC):
-                target = (me, (c + o) % NC)
-                for src, dst, ss, rs in (
-                    (cot_ref, cots, cot_send, cot_recv), (tok_ref, toks, tok_send, tok_recv)
-                ):
-                    copy = pltpu.make_async_remote_copy(
-                        src_ref=src, dst_ref=dst.at[c], send_sem=ss.at[o - 1], recv_sem=rs.at[o - 1],
-                        device_id=target, device_id_type=MESH,
-                    )
-                    copy.start()
-                    extra.append(copy)
+            for o in range(1, 4):
+                spread(c, group[o - 1], o - 1)
+            spread(c, (me, across), 3)
             far = slot_of(1 - near, 0)
-            arrived(far)
-            send(block_copy(far, partner, k_send.at[2]), None)
+            for p in range(PIECES):
+                arrived(far, p)
+                send(block_copy(far, p, partner, k_send.at[2, p]), None)
+
+    for copy in extra[6:8]:
+        copy.wait_recv()
+    for o in range(1, 4):
+        spread(across, group[o - 1], 3 + o)
 
     def lane(e, b):
         return e * 4 + (h if b == 0 else 1 - h) * 2
 
-    def product(rows, b):
+    def product(s, b):
         total = None
         for e in range(2):
             j = lane(e, b)
-            left = jnp.concatenate([emb[j, rows, :], emb[j + 1, rows, :]], axis=1)
+            left = jnp.concatenate(
+                [jnp.concatenate([emb[j + i, pl.ds(r * 128 + s * 64, 64), :] for i in range(2)], axis=1) for r in range(4)],
+                axis=0,
+            )
             at = pl.ds(pl.multiple_of(j * 128, 256), 256)
             right = jnp.concatenate([w_ref[g, at, :] for g in range(3)], axis=1)
             part = jnp.dot(left, right, preferred_element_type=f32)
             total = part if total is None else total + part
-        return total
-
-    for e in range(2):
-        arrived(lane(e, 0) + 1 - k)
-    for q in range(4):
-        rows = pl.ds(q * 128, 128)
-        acc[q] = product(rows, 0)
+        return total.reshape(4, 64, 384)
+
+    for e in range(2):
+        for p in range(PIECES):
+            arrived(lane(e, 0) + 1 - k, p)
+    for s in range(2):
+        acc[s] = product(s, 0)
     far = slot_of(1 - near, 1)
-    arrived(far)
-    send(block_copy(far, partner, k_send.at[3]), None)
-    for e in range(2):
-        arrived(lane(e, 1) + 1 - k)
-
-    q = c % 4
-    base = c - q
+    for p in range(PIECES):
+        arrived(far, p)
+        send(block_copy(far, p, partner, k_send.at[3, p]), None)
+    for e in range(2):
+        for p in range(PIECES):
+            arrived(lane(e, 1) + 1 - k, p)
 
     def part_copy(o, s):
         return pltpu.make_async_remote_copy(
@@ -192,36 +211,31 @@
         )
 
     for s in range(2):
-        for o in (3, 1, 2, 0):
-            group = (q + o) % 4
-            rows = pl.ds(pl.multiple_of(group * 128 + s * 64, 64), 64)
-            half = pl.ds(s * 64, 64)
-            total = acc[group, half, :] + product(rows, 1)
-            if o:
-                part_out[o - 1, s] = total.astype(bf16)
-                part_copy(o, s).start()
-            else:
-                acc[group, half, :] = total
+        acc[s] = acc[s] + product(s, 1)
+        for o in (3, 1, 2):
+            part_out[o - 1, s] = acc[s, (q + o) % 4].astype(bf16)
+            part_copy(o, s).start()
     for s in range(2):
-        half = pl.ds(s * 64, 64)
-        total = acc[q, half, :]
+        total = acc[s, q]
         for o in range(1, 4):
             part_copy(o, s).wait_recv()
             total = total + part_in[o - 1, s].astype(f32)
-        acc[q, half, :] = total
+        acc[s, q] = total
         pair_out[s] = total.astype(bf16)
         pair_copy(s).start()
     for s in range(2):
-        half = pl.ds(s * 64, 64)
         pair_copy(s).wait_recv()
-        table[q, s] = (acc[q, half, :] + pair_in[s].astype(f32)).astype(bf16)
+        table[q, s] = (acc[s, q] + pair_in[s].astype(f32)).astype(bf16)
         for o in (3, 1, 2):
             done_copy(o, s).start()
 
     cots[c] = cot_ref[...]
     toks[c] = tok_ref[...]
-    for copy in extra:
-        copy.wait()
+    for i, copy in enumerate(extra):
+        if 6 <= i < 8:
+            copy.wait_send()
+        else:
+            copy.wait()
     for i in range(NC):
         cotall_ref[i] = cots[i]
         tokall_ref[pl.ds(i, 1), :] = toks[i]
@@ -294,7 +308,7 @@
     lax.fori_loop(0, length, outs, tuple(entering), unroll=4)
 
 
-def mix_kernel(
+def mix(
     p_ref, tok_ref, cot_ref, taps_ref, rates_ref, res_ref,
     mixed_ref, lhs_ref,
     z, filt, cot, drive, glong, lo, gd, gz,
@@ -376,8 +390,10 @@
 SPOT = {0: (0, 0), 1: (1, 0), 2: (0, 1), 3: (1, 1), 4: (2, 1), 5: (3, 1), 6: (2, 0), 7: (3, 0)}
 
 
-def sum_kernel(
-    lhs_ref, w_ref, out_ref,
+def mix_kernel(
+    p_ref, tok_ref, cot_ref, taps_ref, rates_ref, res_ref, w_ref,
+    mixed_ref, pair_ref,
+    z, filt, cot, drive, glong, lo, gd, gz, lhs_ref,
     own, core_out, core_in, first_out, first_in, second_own, second_out, second_in, last_out, last_in,
     core_send, core_recv, first_send, first_recv, second_send, second_recv, last_send, last_recv,
 ):
@@ -400,10 +416,12 @@
     givers = [(flat(x + back_x, (y // 2) * 2 + back_y, e, k), from_c) for e in range(2)]
     loop = jnp.logical_and(dx == 0, dy < 2)
     foreign = [jnp.logical_not(jnp.logical_and(loop, h == e)) for e in range(2)]
-    greet(
-        [(d, None) for d in [partner] + xs + ys] + [(givers[e], foreign[e]) for e in range(2)],
-        9 - loop.astype(jnp.int32),
+    hail([(d, None) for d in [partner] + xs + ys] + [(givers[e], foreign[e]) for e in range(2)])
+    mix(
+        p_ref, tok_ref, cot_ref, taps_ref, rates_ref, res_ref, mixed_ref, lhs_ref,
+        z, filt, cot, drive, glong, lo, gd, gz,
     )
+    pl.semaphore_wait(pltpu.get_barrier_semaphore(), 9 - loop.astype(jnp.int32))
 
     def core_copy(e, a):
         return pltpu.make_async_remote_copy(
@@ -486,7 +504,7 @@
             for i in range(3):
                 both = both + first_in[e, i, b].astype(f32)
             if o:
-                second_out[e, o - 1] = both.astype(bf16)
+                second_out[e, o - 1] = both
                 second_copy(e, o).start()
             else:
                 second_own[e] = both
@@ -494,8 +512,8 @@
         both = second_own[e]
         for o in range(1, 4):
             second_copy(e, o).wait_recv()
-            both = both + second_in[e, o - 1].astype(f32)
-        last_out[e] = both.astype(bf16)
+            both = both + second_in[e, o - 1]
+        last_out[e] = both
 
         @pl.when(foreign[e])
         def _():
@@ -511,7 +529,7 @@
         def _():
             last_wait(e)
 
-    out_ref[...] = (last_in[0].astype(f32) + last_in[1].astype(f32)).astype(bf16)
+    pair_ref[...] = last_in[...]
     for e in range(2):
         for a in range(4):
             core_copy(e, a).wait_send()
@@ -522,6 +540,11 @@
         @pl.when(foreign[e])
         def _():
             last_copy(e).wait_send()
+
+
+def last_kernel(mixed_ref, pair_ref, out_ref, grad_ref):
+    out_ref[...] = mixed_ref[...]
+    grad_ref[...] = (pair_ref[0] + pair_ref[1]).astype(jnp.bfloat16)
 
 
 def on_device(token_ids, embed, w_in, taps, rates, residues, cotangent):
@@ -540,13 +563,13 @@
         out_specs=(VMEM, VMEM, VMEM),
         scratch_shapes=[
             pltpu.VMEM((8, VOCAB, 128), bf16),
-            pltpu.VMEM((4, 128, 384), f32),
+            pltpu.VMEM((2, 4, 64, 384), f32),
             pltpu.VMEM((3, 2, 64, 384), bf16), pltpu.VMEM((3, 2, 64, 384), bf16),
             pltpu.VMEM((2, 64, 384), bf16), pltpu.VMEM((2, 64, 384), bf16),
             pltpu.VMEM((4, 2, 64, 384), bf16),
             pltpu.VMEM((NC, 1, 128), i32),
             pltpu.VMEM((NC, 128, 128), bf16),
-            dma, dma, dma((2, 3)), dma((2, 3)), dma((4,)), dma((8,)),
+            dma, dma((PIECES,)), dma((2, 3, PIECES)), dma((2, 3, PIECES)), dma((4, PIECES)), dma((8, PIECES)),
             dma((3, 2)), dma((3, 2)), dma((2,)), dma((2,)), dma((3, 2)), dma((3, 2)),
             dma((NC - 1,)), dma((NC - 1,)), dma((NC - 1,)), dma((NC - 1,)),
         ],
@@ -554,40 +577,36 @@
         name="table",
     )(embed, w, token_ids.reshape(1, 128), cotangent)
     wide = pltpu.VMEM((1024, 128), f32)
-    mixed, lhs = pl.pallas_call(
+    mixed, pair = pl.pallas_call(
         mix_kernel,
         out_shape=(
             jax.ShapeDtypeStruct((128, 128), bf16),
-            jax.ShapeDtypeStruct((1024, 384), bf16),
+            jax.ShapeDtypeStruct((2, 128, 128), f32),
         ),
-        in_specs=[VMEM] * 6,
+        in_specs=[VMEM] * 7,
         out_specs=(VMEM, VMEM),
         scratch_shapes=[
             pltpu.VMEM((3, 136 * 8, 128), f32), pltpu.VMEM((3, 1024, 128), f32),
             wide, wide, wide, wide, wide,
-            pltpu.VMEM((3, 1024, 128), f32),
-        ],
-        compiler_params=pltpu.CompilerParams(vmem_limit_bytes=LIMIT),
-        name="mix",
-    )(p, toks, cots, taps, rates, residues)
-    own = pl.pallas_call(
-        sum_kernel,
-        out_shape=jax.ShapeDtypeStruct((128, 128), bf16),
-        in_specs=[VMEM, VMEM],
-        out_specs=VMEM,
-        scratch_shapes=[
+            pltpu.VMEM((3, 1024, 128), f32), pltpu.VMEM((1024, 384), bf16),
             pltpu.VMEM((2, 4, 4, 128, 128), f32),
             pltpu.VMEM((2, 4, 4, 128, 128), bf16), pltpu.VMEM((2, 4, 4, 128, 128), bf16),
             pltpu.VMEM((2, 3, 4, 128, 128), bf16), pltpu.VMEM((2, 3, 4, 128, 128), bf16),
             pltpu.VMEM((2, 128, 128), f32),
-            pltpu.VMEM((2, 3, 128, 128), bf16), pltpu.VMEM((2, 3, 128, 128), bf16),
-            pltpu.VMEM((2, 128, 128), bf16), pltpu.VMEM((2, 128, 128), bf16),
+            pltpu.VMEM((2, 3, 128, 128), f32), pltpu.VMEM((2, 3, 128, 128), f32),
+            pltpu.VMEM((2, 128, 128), f32), pltpu.VMEM((2, 128, 128), f32),
             dma((2, 4)), dma((2, 4)), dma((2, 3)), dma((2, 3)), dma((2, 3)), dma((2, 3)), dma((2,)), dma((2,)),
         ],
         compiler_params=pltpu.CompilerParams(collective_id=1, has_side_effects=True, vmem_limit_bytes=LIMIT),
-        name="sums",
-    )(lhs, w)
-    return mixed, own
+        name="mix",
+    )(p, toks, cots, taps, rates, residues, w)
+    return pl.pallas_call(
+        last_kernel,
+        out_shape=(jax.ShapeDtypeStruct((128, 128), bf16), jax.ShapeDtypeStruct((128, 128), bf16)),
+        in_specs=[VMEM, VMEM],
+        out_specs=(VMEM, VMEM),
+        name="last",
+    )(mixed, pair)
 
 
 def solution(mesh):

time: 109 us -> 104 us (0.954)
  the two profiles are of different devices: /device:TPU:5 before, /device:TPU:1 now
where the time goes in v3:
time: 104 us
  Pallas kernels  103 us (99%)
    pallas_call x1, Pallas kernels, on_device(): pl.pallas_call(table_kernel, out_shape=(jax.ShapeDtypeStruct((VOCAB, 384)...  60.5 us
    pallas_call x1, Pallas kernels, on_device(): pl.pallas_call(mix_kernel, out_shape=(jax.ShapeDtypeStruct((128, 128), bf...  41.3 us

profile of v3, /device:TPU:1, one launch (start us, length us, event | category | flops | bytes accessed | tf_op | source)
XLA Modules:
  0.0 104.0 jit_solution(7312803124093859597)
XLA Ops:
  0.6 60.5 %table.1 = (bf16[512,384]{1,0:T(8,128)(2,1)}, s32[8,128]{1,0:T(8,128)}, bf16[8,128,128]{2,1,0:T(8,128)(2,1)}) custom-call(bf16[512,128]{1,0:T(8,128)(2,1)} %embed_ref.1, bf16[3,1024,128]{2,1,0:T(8,128)(2,1)} %bitcast.3, s32[1,128]{1,0:T(1,128)} %bitcast.6, bf16[128,128]{1,0:T(8,128)(2,1)} %cot_ref.1), custom_call_target="tpu_custom_call" | custom-call | tf_op jit(solution)/shard_map/table/pallas_call | solution.py:555
  61.1 41.3 %mix.1 = (bf16[128,128]{1,0:T(8,128)(2,1)}, f32[2,128,128]{2,1,0:T(8,128)}) custom-call(bf16[512,384]{1,0:T(8,128)(2,1)} %get-tuple-element.7.p_ref, s32[8,128]{1,0:T(8,128)} %get-tuple-element.8.tok_ref, bf16[8,128,128]{2,1,0:T(8,128)(2,1)} %get-tuple-element.9.cot_ref, f32[3,7,128]{2,1,0:T(8,128)} %bitcast.5, f32[16,128]{1,0:T(8,128)} %rates_ref.1, ...), custom_call_target="tpu_custom_call" | custom-call | tf_op jit(solution)/shard_map/mix/pallas_call | solution.py:580
  102.4 1.6 %last.1 = (bf16[128,128]{1,0:T(8,128)(2,1)}, bf16[128,128]{1,0:T(8,128)(2,1)}) custom-call(bf16[128,128]{1,0:T(8,128)(2,1)} %get-tuple-element.10.mixed_ref, f32[2,128,128]{2,1,0:T(8,128)} %get-tuple-element.11.pair_ref), custom_call_target="tpu_custom_call" | custom-call | tf_op jit(solution)/shard_map/last/pallas_call | solution.py:603

commit v4 on v3

--- a/solution.py
+++ b/solution.py
@@ -12,8 +12,8 @@
 ANY = pl.BlockSpec(memory_space=pl.ANY)
 LIMIT = 60 * 1024 * 1024
 NC = 8
-PIECES = 2
-PIECE = 256
+CHIPS = 16
+PIECE = 32
 VOCAB = 512
 MODES = 16
 TAPS = 7
@@ -49,77 +49,95 @@
 def table_kernel(
     embed_ref, w_ref, tok_ref, cot_ref,
     p_ref, tokall_ref, cotall_ref,
-    emb, acc, part_out, part_in, pair_out, pair_in, table, toks, cots,
-    local_sem, half_send, x_send, y_send, k_send, a_recv,
+    emb, stage, acc, part_out, part_in, pair_out, pair_in, table, toks, cots,
+    local_sem, half_send, half_recv, scat_send, scat_recv, all_send, all_recv, core_send, core_recv,
     part_send, part_recv, pair_send, pair_recv, done_send, done_recv,
     cot_send, cot_recv, tok_send, tok_recv,
 ):
     f32, bf16 = jnp.float32, jnp.bfloat16
     x, y, h, k, c = place()
     me = flat(x, y, h, k)
+    spot = x * 4 + y
     mine = 2 * x + y // 2
     yb = y % 2
     edge = jnp.where(mine < NC // 2, NC - 1, 0)
-    x0, y0 = c // 2, (c % 2) * 2
-    dy = (y - y0 + 4) % 4
-    on_row = dy < 2
     source = mine == c
-    near = jnp.where(dy == 1, 1, 0)
-    own = yb * 4 + h * 2 + k
-
-    xs = [flat(x + o, y, h, k) for o in range(1, 4)]
-    ys = [flat(x, y + o, h, k) for o in range(1, 4)]
+    gives = c == edge
     partner = flat(x, y, h, 1 - k)
     other = flat(x, y, 1 - h, k)
-    gives = c == edge
     q = c % 4
     base = c - q
     across = (c + 4) % NC
     group = [(me, base + (q + o) % 4) for o in range(1, 4)]
+
+    def chip(i):
+        return flat(i // 4, i % 4, h, k)
+
     greet(
-        [((d, c), None) for d in xs + ys + [partner]]
+        [((chip((spot + o) % CHIPS), c), None) for o in range(1, CHIPS)]
+        + [((partner, c), None)]
         + [(d, None) for d in group + [(me, across)]]
         + [((other, edge), source)],
-        11 + gives.astype(jnp.int32),
+        CHIPS + 4 + gives.astype(jnp.int32),
     )
 
-    local = pltpu.make_async_copy(embed_ref, emb.at[own], local_sem)
-
-    def block_copy(slot, p, target, sem, src=None, to=c):
-        rows = pl.ds(p * PIECE, PIECE)
-        return pltpu.make_async_remote_copy(
-            src_ref=emb.at[slot, rows] if src is None else src.at[rows], dst_ref=emb.at[slot, rows], send_sem=sem,
-            recv_sem=a_recv.at[slot, p], device_id=(target, to), device_id_type=MESH,
-        )
-
-    def arrived(slot, p):
-        block_copy(slot, p, partner, k_send.at[0, 0]).wait_recv()
-
-    sends = []
-
-    def send(copy, when):
-        sends.append((copy, when))
-        if when is None:
-            copy.start()
-        else:
-
-            @pl.when(when)
-            def _():
-                copy.start()
-
-    for p in range(PIECES):
-        send(block_copy(own, p, other, half_send.at[p], embed_ref, mine), gives)
-    for p in range(PIECES):
-        for o in (2, 1, 3):
-            send(block_copy(own, p, xs[o - 1], x_send.at[0, o - 1, p], embed_ref), source)
+    def half_copy(m):
+        rows = pl.ds(m * 128, 128)
+        return pltpu.make_async_remote_copy(
+            src_ref=embed_ref.at[rows], dst_ref=stage.at[rows], send_sem=half_send.at[m], recv_sem=half_recv.at[m],
+            device_id=(other, mine), device_id_type=MESH,
+        )
+
+    def side(b):
+        return h if b == 0 else 1 - h
+
+    def scat_copy(b, i, row):
+        rows = pl.ds(pl.multiple_of(i * PIECE, PIECE), PIECE)
+        return pltpu.make_async_remote_copy(
+            src_ref=(embed_ref if b == 0 else stage).at[rows], dst_ref=emb.at[i, side(b), k, row],
+            send_sem=scat_send.at[b, i], recv_sem=scat_recv.at[b, row], device_id=(chip(i), c), device_id_type=MESH,
+        )
+
+    def own_copy(b):
+        rows = pl.ds(pl.multiple_of(spot * PIECE, PIECE), PIECE)
+        return pltpu.make_async_copy(
+            (embed_ref if b == 0 else stage).at[rows], emb.at[spot, side(b), k, yb], local_sem.at[b]
+        )
+
+    def all_copy(b, o):
+        return pltpu.make_async_remote_copy(
+            src_ref=emb.at[spot, side(b), k], dst_ref=emb.at[spot, side(b), k], send_sem=all_send.at[b, o],
+            recv_sem=all_recv.at[b, o], device_id=(chip((spot + o) % CHIPS), c), device_id_type=MESH,
+        )
+
+    def core_copy(b, o):
+        i = (spot + CHIPS - o) % CHIPS
+        return pltpu.make_async_remote_copy(
+            src_ref=emb.at[i, side(b), k], dst_ref=emb.at[i, side(b), k], send_sem=core_send.at[b, o],
+            recv_sem=core_recv.at[b, o], device_id=(partner, c), device_id_type=MESH,
+        )
+
+    def each(first, last, body):
+        def step(i, _):
+            body(i)
+            return 0
+
+        lax.fori_loop(first, last, step, 0)
+
+    @pl.when(gives)
+    def _():
+        for m in range(4):
+            half_copy(m).start()
+
+    def scatter(b, o):
+        i = (spot + o) % CHIPS
+        scat_copy(b, i, yb).start()
 
     @pl.when(source)
     def _():
-        local.start()
-        local.wait()
-
-    def slot_of(row, b):
-        return row * 4 + (h if b == 0 else 1 - h) * 2 + k
+        each(1, CHIPS, lambda o: scatter(0, o))
+        own_copy(0).start()
+        own_copy(0).wait()
 
     extra = []
 
@@ -132,65 +150,67 @@
             copy.start()
             extra.append(copy)
 
-    for b in range(2):
-        slot = slot_of(near, b)
-        for p in range(PIECES):
-            if b == 0:
-
-                @pl.when(jnp.logical_not(source))
+    def share(b):
+        for row in range(2):
+
+            @pl.when(jnp.logical_not(jnp.logical_and(source, yb == row)))
+            def _():
+                scat_copy(b, spot, row).wait_recv()
+
+        each(1, CHIPS, lambda o: all_copy(b, o).start())
+        core_copy(b, 0).start()
+
+    def gathered(b, o):
+        all_copy(b, o).wait_recv()
+        core_copy(b, o).start()
+
+    share(0)
+
+    @pl.when(source)
+    def _():
+        for m in range(4):
+            half_copy(m).wait_recv()
+            for i in range(m * 4, m * 4 + 4):
+
+                @pl.when(i != spot)
                 def _():
-                    arrived(slot, p)
-
-            else:
-                arrived(slot, p)
-                for o in (2, 1, 3):
-                    send(block_copy(slot, p, xs[o - 1], x_send.at[1, o - 1, p]), source)
-            for o in (2, 1, 3):
-                send(block_copy(slot, p, ys[o - 1], y_send.at[b, o - 1, p]), on_row)
-            send(block_copy(slot, p, partner, k_send.at[b, p]), None)
-        if b == 0:
-            for o in range(1, 4):
-                spread(c, group[o - 1], o - 1)
-            spread(c, (me, across), 3)
-            far = slot_of(1 - near, 0)
-            for p in range(PIECES):
-                arrived(far, p)
-                send(block_copy(far, p, partner, k_send.at[2, p]), None)
-
+                    scat_copy(1, i, yb).start()
+
+        own_copy(1).start()
+        own_copy(1).wait()
+
+    for o in range(1, 4):
+        spread(c, group[o - 1], o - 1)
+    spread(c, (me, across), 3)
+    share(1)
+    each(1, CHIPS, lambda o: gathered(0, o))
     for copy in extra[6:8]:
         copy.wait_recv()
     for o in range(1, 4):
         spread(across, group[o - 1], 3 + o)
 
-    def lane(e, b):
-        return e * 4 + (h if b == 0 else 1 - h) * 2
-
     def product(s, b):
         total = None
+        hb = side(b)
         for e in range(2):
-            j = lane(e, b)
             left = jnp.concatenate(
-                [jnp.concatenate([emb[j + i, pl.ds(r * 128 + s * 64, 64), :] for i in range(2)], axis=1) for r in range(4)],
+                [
+                    jnp.concatenate([emb[s * 8 + i, hb, kk, e] for kk in range(2)], axis=1)
+                    for i in range(8)
+                ],
                 axis=0,
             )
-            at = pl.ds(pl.multiple_of(j * 128, 256), 256)
+            at = pl.ds(pl.multiple_of(e * 512 + hb * 256, 256), 256)
             right = jnp.concatenate([w_ref[g, at, :] for g in range(3)], axis=1)
             part = jnp.dot(left, right, preferred_element_type=f32)
             total = part if total is None else total + part
         return total.reshape(4, 64, 384)
 
-    for e in range(2):
-        for p in range(PIECES):
-            arrived(lane(e, 0) + 1 - k, p)
+    each(0, CHIPS, lambda o: core_copy(0, o).wait_recv())
     for s in range(2):
         acc[s] = product(s, 0)
-    far = slot_of(1 - near, 1)
-    for p in range(PIECES):
-        arrived(far, p)
-        send(block_copy(far, p, partner, k_send.at[3, p]), None)
-    for e in range(2):
-        for p in range(PIECES):
-            arrived(lane(e, 1) + 1 - k, p)
+    each(1, CHIPS, lambda o: gathered(1, o))
+    each(0, CHIPS, lambda o: core_copy(1, o).wait_recv())
 
     def part_copy(o, s):
         return pltpu.make_async_remote_copy(
@@ -239,14 +259,19 @@
     for i in range(NC):
         cotall_ref[i] = cots[i]
         tokall_ref[pl.ds(i, 1), :] = toks[i]
-    for copy, when in sends:
-        if when is None:
-            copy.wait_send()
-        else:
-
-            @pl.when(when)
-            def _():
-                copy.wait_send()
+    for b in range(2):
+        each(1, CHIPS, lambda o: all_copy(b, o).wait_send())
+        each(0, CHIPS, lambda o: core_copy(b, o).wait_send())
+
+    @pl.when(source)
+    def _():
+        for b in range(2):
+            each(1, CHIPS, lambda o: scat_copy(b, (spot + o) % CHIPS, yb).wait_send())
+
+    @pl.when(gives)
+    def _():
+        for m in range(4):
+            half_copy(m).wait_send()
 
     for s in range(2):
         pair_copy(s).wait_send()
@@ -255,7 +280,7 @@
             done_copy(o, s).wait()
     for i in range(4):
         for s in range(2):
-            p_ref[pl.ds(i * 128 + s * 64, 64), :] = table[i, s]
+            p_ref[pl.ds(s * 256 + i * 64, 64), :] = table[i, s]
 
 
 def shifted_up(value, by, row):
@@ -394,16 +419,20 @@
     p_ref, tok_ref, cot_ref, taps_ref, rates_ref, res_ref, w_ref,
     mixed_ref, pair_ref,
     z, filt, cot, drive, glong, lo, gd, gz, lhs_ref,
-    own, core_out, core_in, first_out, first_in, second_own, second_out, second_in, last_out, last_in,
-    core_send, core_recv, first_send, first_recv, second_send, second_recv, last_send, last_recv,
+    own, core_out, core_in, rest_out, rest_in, last_out, last_in,
+    core_send, core_recv, rest_send, rest_recv, last_send, last_recv,
 ):
     f32, bf16 = jnp.float32, jnp.bfloat16
     x, y, h, k, c = place()
     x0, y0 = c // 2, (c % 2) * 2
     dx, dy = (x - x0 + 4) % 4, (y - y0 + 4) % 4
     partner = (flat(x, y, h, 1 - k), c)
-    xs = [(flat(x + o, y, h, k), c) for o in range(1, 4)]
-    ys = [(flat(x, y + o, h, k), c) for o in range(1, 4)]
+    spot = x * 4 + y
+
+    def chip(o):
+        i = (spot + o) % CHIPS
+        return i // 4, i % 4
+
     yb = jnp.where(jnp.logical_or(dy == 1, dy == 2), 1, 0)
     far = jnp.where(dy >= 2, 1, 0)
     step = jnp.where(dx < 2, dx + 2 * far, dx + 4 - 2 * far)
@@ -416,34 +445,29 @@
     givers = [(flat(x + back_x, (y // 2) * 2 + back_y, e, k), from_c) for e in range(2)]
     loop = jnp.logical_and(dx == 0, dy < 2)
     foreign = [jnp.logical_not(jnp.logical_and(loop, h == e)) for e in range(2)]
-    hail([(d, None) for d in [partner] + xs + ys] + [(givers[e], foreign[e]) for e in range(2)])
+    plane = [(flat(*chip(o), h, k), c) for o in range(1, CHIPS)]
+    hail([(d, None) for d in [partner] + plane] + [(givers[e], foreign[e]) for e in range(2)])
     mix(
         p_ref, tok_ref, cot_ref, taps_ref, rates_ref, res_ref, mixed_ref, lhs_ref,
         z, filt, cot, drive, glong, lo, gd, gz,
     )
-    pl.semaphore_wait(pltpu.get_barrier_semaphore(), 9 - loop.astype(jnp.int32))
+    pl.semaphore_wait(pltpu.get_barrier_semaphore(), CHIPS + 2 - loop.astype(jnp.int32))
 
     def core_copy(e, a):
         return pltpu.make_async_remote_copy(
-            src_ref=core_out.at[e, a], dst_ref=core_in.at[e, a],
+            src_ref=core_out.at[e, pl.ds(a * 4, 4)], dst_ref=core_in.at[e, pl.ds(a * 4, 4)],
             send_sem=core_send.at[e, a], recv_sem=core_recv.at[e, a], device_id=partner, device_id_type=MESH,
         )
 
-    spots = [dx, dy]
-    lines = [xs, ys]
-
-    def first_copy(e, o):
-        return pltpu.make_async_remote_copy(
-            src_ref=first_out.at[e, o - 1], dst_ref=first_in.at[e, o - 1],
-            send_sem=first_send.at[e, o - 1], recv_sem=first_recv.at[e, o - 1],
-            device_id=lines[e][o - 1], device_id_type=MESH,
-        )
-
-    def second_copy(e, o):
-        return pltpu.make_async_remote_copy(
-            src_ref=second_out.at[e, o - 1], dst_ref=second_in.at[e, o - 1],
-            send_sem=second_send.at[e, o - 1], recv_sem=second_recv.at[e, o - 1],
-            device_id=lines[1 - e][o - 1], device_id_type=MESH,
+    def slot(o):
+        cx, cy = chip(o)
+        return ((cx - x0 + 4) % 4) * 4 + (cy - y0 + 4) % 4
+
+    def rest_copy(e, o):
+        return pltpu.make_async_remote_copy(
+            src_ref=rest_out.at[e, o], dst_ref=rest_in.at[e, o],
+            send_sem=rest_send.at[e, o], recv_sem=rest_recv.at[e, o],
+            device_id=(flat(*chip(o), h, k), c), device_id_type=MESH,
         )
 
     def last_copy(e):
@@ -468,14 +492,13 @@
             sx, sfar = SPOT[s]
             for r in range(2):
                 sy = 3 * sfar if r == 0 else 1 + sfar
-                a, b = (sx, sy) if e == 0 else (sy, sx)
-                store(e, a, b, out[s * 128 : (s + 1) * 128, r * 128 : (r + 1) * 128])
-
-    def to_core(e, a, b, value):
-        core_out[e, a, b] = value.astype(bf16)
-
-    def to_own(e, a, b, value):
-        own[e, a, b] = value
+                store(e, sx * 4 + sy, out[s * 128 : (s + 1) * 128, r * 128 : (r + 1) * 128])
+
+    def to_core(e, a, value):
+        core_out[e, a] = value.astype(bf16)
+
+    def to_own(e, a, value):
+        own[e, a] = value
 
     for e in range(2):
         tile(e, 1 - k, to_core)
@@ -483,36 +506,24 @@
             core_copy(e, a).start()
     for e in range(2):
         tile(e, k, to_own)
-    order = [2, 1, 3, 0]
-    for o in order:
-        for e in range(2):
-            a = (spots[e] + o) % 4
+        for a in range(4):
             core_copy(e, a).wait_recv()
-            both = own[e, a] + core_in[e, a].astype(f32)
-            if o:
-                first_out[e, o - 1] = both.astype(bf16)
-                first_copy(e, o).start()
-            else:
-                own[e, a] = both
+
+        def give(o, _):
+            a = slot(o)
+            rest_out[e, o] = (own[e, a] + core_in[e, a].astype(f32)).astype(bf16)
+            rest_copy(e, o).start()
+            return 0
+
+        lax.fori_loop(1, CHIPS, give, 0)
     for e in range(2):
-        for o in range(1, 4):
-            first_copy(e, o).wait_recv()
-    for o in order:
-        for e in range(2):
-            b = (spots[1 - e] + o) % 4
-            both = own[e, spots[e], b]
-            for i in range(3):
-                both = both + first_in[e, i, b].astype(f32)
-            if o:
-                second_out[e, o - 1] = both
-                second_copy(e, o).start()
-            else:
-                second_own[e] = both
-    for e in range(2):
-        both = second_own[e]
-        for o in range(1, 4):
-            second_copy(e, o).wait_recv()
-            both = both + second_in[e, o - 1]
+
+        def take(o, both):
+            rest_copy(e, o).wait_recv()
+            return both + rest_in[e, o].astype(f32)
+
+        home = dx * 4 + dy
+        both = lax.fori_loop(1, CHIPS, take, own[e, home] + core_in[e, home].astype(f32))
         last_out[e] = both
 
         @pl.when(foreign[e])
@@ -533,9 +544,12 @@
     for e in range(2):
         for a in range(4):
             core_copy(e, a).wait_send()
-        for o in range(1, 4):
-            first_copy(e, o).wait_send()
-            second_copy(e, o).wait_send()
+
+        def sent(o, _):
+            rest_copy(e, o).wait_send()
+            return 0
+
+        lax.fori_loop(1, CHIPS, sent, 0)
 
         @pl.when(foreign[e])
         def _():
@@ -562,14 +576,16 @@
         in_specs=[ANY, VMEM, VMEM, VMEM],
         out_specs=(VMEM, VMEM, VMEM),
         scratch_shapes=[
-            pltpu.VMEM((8, VOCAB, 128), bf16),
+            pltpu.VMEM((CHIPS, 2, 2, 2, PIECE, 128), bf16),
+            pltpu.VMEM((VOCAB, 128), bf16),
             pltpu.VMEM((2, 4, 64, 384), f32),
             pltpu.VMEM((3, 2, 64, 384), bf16), pltpu.VMEM((3, 2, 64, 384), bf16),
             pltpu.VMEM((2, 64, 384), bf16), pltpu.VMEM((2, 64, 384), bf16),
             pltpu.VMEM((4, 2, 64, 384), bf16),
             pltpu.VMEM((NC, 1, 128), i32),
             pltpu.VMEM((NC, 128, 128), bf16),
-            dma, dma((PIECES,)), dma((2, 3, PIECES)), dma((2, 3, PIECES)), dma((4, PIECES)), dma((8, PIECES)),
+            dma((2,)), dma((4,)), dma((4,)), dma((2, CHIPS)), dma((2, 2)),
+            dma((2, CHIPS)), dma((2, CHIPS)), dma((2, CHIPS)), dma((2, CHIPS)),
             dma((3, 2)), dma((3, 2)), dma((2,)), dma((2,)), dma((3, 2)), dma((3, 2)),
             dma((NC - 1,)), dma((NC - 1,)), dma((NC - 1,)), dma((NC - 1,)),
         ],
@@ -589,13 +605,11 @@
             pltpu.VMEM((3, 136 * 8, 128), f32), pltpu.VMEM((3, 1024, 128), f32),
             wide, wide, wide, wide, wide,
             pltpu.VMEM((3, 1024, 128), f32), pltpu.VMEM((1024, 384), bf16),
-            pltpu.VMEM((2, 4, 4, 128, 128), f32),
-            pltpu.VMEM((2, 4, 4, 128, 128), bf16), pltpu.VMEM((2, 4, 4, 128, 128), bf16),
-            pltpu.VMEM((2, 3, 4, 128, 128), bf16), pltpu.VMEM((2, 3, 4, 128, 128), bf16),
-            pltpu.VMEM((2, 128, 128), f32),
-            pltpu.VMEM((2, 3, 128, 128), f32), pltpu.VMEM((2, 3, 128, 128), f32),
+            pltpu.VMEM((2, CHIPS, 128, 128), f32),
+            pltpu.VMEM((2, CHIPS, 128, 128), bf16), pltpu.VMEM((2, CHIPS, 128, 128), bf16),
+            pltpu.VMEM((2, CHIPS, 128, 128), bf16), pltpu.VMEM((2, CHIPS, 128, 128), bf16),
             pltpu.VMEM((2, 128, 128), f32), pltpu.VMEM((2, 128, 128), f32),
-            dma((2, 4)), dma((2, 4)), dma((2, 3)), dma((2, 3)), dma((2, 3)), dma((2, 3)), dma((2,)), dma((2,)),
+            dma((2, 4)), dma((2, 4)), dma((2, CHIPS)), dma((2, CHIPS)), dma((2,)), dma((2,)),
         ],
         compiler_params=pltpu.CompilerParams(collective_id=1, has_side_effects=True, vmem_limit_bytes=LIMIT),
         name="mix",

time: 104 us -> 102 us (0.981)
  the two profiles are of different devices: /device:TPU:1 before, /device:TPU:385 now
where the time goes in v4:
time: 102 us
  Pallas kernels  101 us (99%)
    pallas_call x1, Pallas kernels, on_device(): pl.pallas_call(table_kernel, out_shape=(jax.ShapeDtypeStruct((VOCAB, 384)...  51.2 us
    pallas_call x1, Pallas kernels, on_device(): pl.pallas_call(mix_kernel, out_shape=(jax.ShapeDtypeStruct((128, 128), bf...  48.6 us

profile of v4, /device:TPU:385, one launch (start us, length us, event | category | flops | bytes accessed | tf_op | source)
XLA Modules:
  0.0 102.0 jit_solution(284871745430813192)
XLA Ops:
  0.6 51.2 %table.1 = (bf16[512,384]{1,0:T(8,128)(2,1)}, s32[8,128]{1,0:T(8,128)}, bf16[8,128,128]{2,1,0:T(8,128)(2,1)}) custom-call(bf16[512,128]{1,0:T(8,128)(2,1)} %embed_ref.1, bf16[3,1024,128]{2,1,0:T(8,128)(2,1)} %bitcast.3, s32[1,128]{1,0:T(1,128)} %bitcast.6, bf16[128,128]{1,0:T(8,128)(2,1)} %cot_ref.1), custom_call_target="tpu_custom_call" | custom-call | tf_op jit(solution)/shard_map/table/pallas_call | solution.py:569
  51.8 48.6 %mix.1 = (bf16[128,128]{1,0:T(8,128)(2,1)}, f32[2,128,128]{2,1,0:T(8,128)}) custom-call(bf16[512,384]{1,0:T(8,128)(2,1)} %get-tuple-element.7.p_ref, s32[8,128]{1,0:T(8,128)} %get-tuple-element.8.tok_ref, bf16[8,128,128]{2,1,0:T(8,128)(2,1)} %get-tuple-element.9.cot_ref, f32[3,7,128]{2,1,0:T(8,128)} %bitcast.5, f32[16,128]{1,0:T(8,128)} %rates_ref.1, ...), custom_call_target="tpu_custom_call" | custom-call | tf_op jit(solution)/shard_map/mix/pallas_call | solution.py:596
  100.4 1.6 %last.1 = (bf16[128,128]{1,0:T(8,128)(2,1)}, bf16[128,128]{1,0:T(8,128)(2,1)}) custom-call(bf16[128,128]{1,0:T(8,128)(2,1)} %get-tuple-element.10.mixed_ref, f32[2,128,128]{2,1,0:T(8,128)} %get-tuple-element.11.pair_ref), custom_call_target="tpu_custom_call" | custom-call | tf_op jit(solution)/shard_map/last/pallas_call | solution.py:617

commit v5 on v4

--- a/solution.py
+++ b/solution.py
@@ -46,9 +46,8 @@
     pl.semaphore_wait(pltpu.get_barrier_semaphore(), count)
 
 
-def table_kernel(
-    embed_ref, w_ref, tok_ref, cot_ref,
-    p_ref, tokall_ref, cotall_ref,
+def build_table(
+    friends, count, embed_ref, w_ref, w_copy, tok_ref, cot_ref,
     emb, stage, acc, part_out, part_in, pair_out, pair_in, table, toks, cots,
     local_sem, half_send, half_recv, scat_send, scat_recv, all_send, all_recv, core_send, core_recv,
     part_send, part_recv, pair_send, pair_recv, done_send, done_recv,
@@ -77,8 +76,9 @@
         [((chip((spot + o) % CHIPS), c), None) for o in range(1, CHIPS)]
         + [((partner, c), None)]
         + [(d, None) for d in group + [(me, across)]]
-        + [((other, edge), source)],
-        CHIPS + 4 + gives.astype(jnp.int32),
+        + [((other, edge), source)]
+        + friends,
+        CHIPS + 4 + gives.astype(jnp.int32) + count,
     )
 
     def half_copy(m):
@@ -207,6 +207,7 @@
         return total.reshape(4, 64, 384)
 
     each(0, CHIPS, lambda o: core_copy(0, o).wait_recv())
+    w_copy.wait()
     for s in range(2):
         acc[s] = product(s, 0)
     each(1, CHIPS, lambda o: gathered(1, o))
@@ -226,7 +227,7 @@
 
     def done_copy(o, s):
         return pltpu.make_async_remote_copy(
-            src_ref=table.at[q, s], dst_ref=table.at[q, s], send_sem=done_send.at[o - 1, s],
+            src_ref=table.at[s, q], dst_ref=table.at[s, q], send_sem=done_send.at[o - 1, s],
             recv_sem=done_recv.at[o - 1, s], device_id=(me, base + (q + o) % 4), device_id_type=MESH,
         )
 
@@ -245,42 +246,43 @@
         pair_copy(s).start()
     for s in range(2):
         pair_copy(s).wait_recv()
-        table[q, s] = (acc[s, q] + pair_in[s].astype(f32)).astype(bf16)
+        table[s, q] = (acc[s, q] + pair_in[s].astype(f32)).astype(bf16)
         for o in (3, 1, 2):
             done_copy(o, s).start()
 
     cots[c] = cot_ref[...]
     toks[c] = tok_ref[...]
     for i, copy in enumerate(extra):
-        if 6 <= i < 8:
+        if not 6 <= i < 8:
+            copy.wait_recv()
+    for s in range(2):
+        for o in range(1, 4):
+            done_copy(o, s).wait_recv()
+
+    def finish():
+        for copy in extra:
             copy.wait_send()
-        else:
-            copy.wait()
-    for i in range(NC):
-        cotall_ref[i] = cots[i]
-        tokall_ref[pl.ds(i, 1), :] = toks[i]
-    for b in range(2):
-        each(1, CHIPS, lambda o: all_copy(b, o).wait_send())
-        each(0, CHIPS, lambda o: core_copy(b, o).wait_send())
-
-    @pl.when(source)
-    def _():
         for b in range(2):
-            each(1, CHIPS, lambda o: scat_copy(b, (spot + o) % CHIPS, yb).wait_send())
-
-    @pl.when(gives)
-    def _():
-        for m in range(4):
-            half_copy(m).wait_send()
-
-    for s in range(2):
-        pair_copy(s).wait_send()
-        for o in range(1, 4):
-            part_copy(o, s).wait_send()
-            done_copy(o, s).wait()
-    for i in range(4):
+            each(1, CHIPS, lambda o: all_copy(b, o).wait_send())
+            each(0, CHIPS, lambda o: core_copy(b, o).wait_send())
+
+        @pl.when(source)
+        def _():
+            for b in range(2):
+                each(1, CHIPS, lambda o: scat_copy(b, (spot + o) % CHIPS, yb).wait_send())
+
+        @pl.when(gives)
+        def _():
+            for m in range(4):
+                half_copy(m).wait_send()
+
         for s in range(2):
-            p_ref[pl.ds(s * 256 + i * 64, 64), :] = table[i, s]
+            pair_copy(s).wait_send()
+            for o in range(1, 4):
+                part_copy(o, s).wait_send()
+                done_copy(o, s).wait_send()
+
+    return finish
 
 
 def shifted_up(value, by, row):
@@ -334,7 +336,7 @@
 
 
 def mix(
-    p_ref, tok_ref, cot_ref, taps_ref, rates_ref, res_ref,
+    table, toks, cots, taps_ref, rates_ref, res_ref,
     mixed_ref, lhs_ref,
     z, filt, cot, drive, glong, lo, gd, gz,
 ):
@@ -344,21 +346,24 @@
     lane = lax.broadcasted_iota(jnp.int32, (8, VOCAB), 1)
 
     for s in range(NC):
-        cot[pl.ds(s, 128, stride=8), :] = cot_ref[s].astype(jnp.float32)
-
-    def pick(i, toks):
+        cot[pl.ds(s, 128, stride=8), :] = cots[s].astype(jnp.float32)
+
+    ids = jnp.concatenate([toks[i] for i in range(NC)], axis=0)
+    whole = table[...].reshape(VOCAB, 384)
+
+    def pick(i, ids):
         rows = []
         for j in range(0, 16, 2):
-            two = [jnp.where(toks[:, j + e : j + e + 1] == lane, 1.0, 0.0) for e in range(2)]
+            two = [jnp.where(ids[:, j + e : j + e + 1] == lane, 1.0, 0.0) for e in range(2)]
             rows.append(jnp.concatenate(two, axis=0).astype(jnp.bfloat16))
         hot = jnp.concatenate(rows, axis=0)
-        found = jnp.dot(hot, p_ref[...], preferred_element_type=jnp.float32)
+        found = jnp.dot(hot, whole, preferred_element_type=jnp.float32)
         start = pl.ds(pl.multiple_of((halo + i * 16) * 8, 128 // 2), 128)
         for g in range(3):
             z[g, start, :] = found[:, g * 128 : (g + 1) * 128]
-        return pltpu.roll(toks, 112, 1)
-
-    lax.fori_loop(0, 8, pick, tok_ref[...])
+        return pltpu.roll(ids, 112, 1)
+
+    lax.fori_loop(0, 8, pick, ids)
     for g in range(3):
         for d in range(1, TAPS):
             z[g, pl.ds((halo - d) * 8, 8), :] = shifted_up(z[g, pl.ds((halo + 128 - d) * 8, 8), :], 1, row)
@@ -415,13 +420,20 @@
 SPOT = {0: (0, 0), 1: (1, 0), 2: (0, 1), 3: (1, 1), 4: (2, 1), 5: (3, 1), 6: (2, 0), 7: (3, 0)}
 
 
-def mix_kernel(
-    p_ref, tok_ref, cot_ref, taps_ref, rates_ref, res_ref, w_ref,
+def whole_kernel(
+    embed_ref, w_hbm, tok_ref, cot_ref, taps_ref, rates_ref, res_ref,
     mixed_ref, pair_ref,
+    w_ref, w_sem,
+    emb, stage, acc, part_out, part_in, pair_out, pair_in, table, toks, cots,
+    local_sem, half_send, half_recv, scat_send, scat_recv, all_send, all_recv, swap_send, swap_recv,
+    part_send, part_recv, pair_send, pair_recv, done_send, done_recv,
+    cot_send, cot_recv, tok_send, tok_recv,
     z, filt, cot, drive, glong, lo, gd, gz, lhs_ref,
     own, core_out, core_in, rest_out, rest_in, last_out, last_in,
     core_send, core_recv, rest_send, rest_recv, last_send, last_recv,
 ):
+    w_copy = pltpu.make_async_copy(w_hbm, w_ref, w_sem)
+    w_copy.start()
     f32, bf16 = jnp.float32, jnp.bfloat16
     x, y, h, k, c = place()
     x0, y0 = c // 2, (c % 2) * 2
@@ -445,13 +457,18 @@
     givers = [(flat(x + back_x, (y // 2) * 2 + back_y, e, k), from_c) for e in range(2)]
     loop = jnp.logical_and(dx == 0, dy < 2)
     foreign = [jnp.logical_not(jnp.logical_and(loop, h == e)) for e in range(2)]
-    plane = [(flat(*chip(o), h, k), c) for o in range(1, CHIPS)]
-    hail([(d, None) for d in [partner] + plane] + [(givers[e], foreign[e]) for e in range(2)])
+    finish = build_table(
+        [(givers[e], foreign[e]) for e in range(2)], 2 - loop.astype(jnp.int32),
+        embed_ref, w_ref, w_copy, tok_ref, cot_ref,
+        emb, stage, acc, part_out, part_in, pair_out, pair_in, table, toks, cots,
+        local_sem, half_send, half_recv, scat_send, scat_recv, all_send, all_recv, swap_send, swap_recv,
+        part_send, part_recv, pair_send, pair_recv, done_send, done_recv,
+        cot_send, cot_recv, tok_send, tok_recv,
+    )
     mix(
-        p_ref, tok_ref, cot_ref, taps_ref, rates_ref, res_ref, mixed_ref, lhs_ref,
+        table, toks, cots, taps_ref, rates_ref, res_ref, mixed_ref, lhs_ref,
         z, filt, cot, drive, glong, lo, gd, gz,
     )
-    pl.semaphore_wait(pltpu.get_barrier_semaphore(), CHIPS + 2 - loop.astype(jnp.int32))
 
     def core_copy(e, a):
         return pltpu.make_async_remote_copy(
@@ -524,7 +541,7 @@
 
         home = dx * 4 + dy
         both = lax.fori_loop(1, CHIPS, take, own[e, home] + core_in[e, home].astype(f32))
-        last_out[e] = both
+        last_out[e] = both.astype(bf16)
 
         @pl.when(foreign[e])
         def _():
@@ -541,6 +558,7 @@
             last_wait(e)
 
     pair_ref[...] = last_in[...]
+    finish()
     for e in range(2):
         for a in range(4):
             core_copy(e, a).wait_send()
@@ -558,7 +576,7 @@
 
 def last_kernel(mixed_ref, pair_ref, out_ref, grad_ref):
     out_ref[...] = mixed_ref[...]
-    grad_ref[...] = (pair_ref[0] + pair_ref[1]).astype(jnp.bfloat16)
+    grad_ref[...] = (pair_ref[0].astype(jnp.float32) + pair_ref[1].astype(jnp.float32)).astype(jnp.bfloat16)
 
 
 def on_device(token_ids, embed, w_in, taps, rates, residues, cotangent):
@@ -566,54 +584,41 @@
     dma = pltpu.SemaphoreType.DMA
     w = w_in.transpose(1, 0, 2)
     taps = taps.transpose(1, 0, 2)
-    p, toks, cots = pl.pallas_call(
-        table_kernel,
+    wide = pltpu.VMEM((1024, 128), f32)
+    mixed, pair = pl.pallas_call(
+        whole_kernel,
         out_shape=(
-            jax.ShapeDtypeStruct((VOCAB, 384), bf16),
-            jax.ShapeDtypeStruct((NC, 128), i32),
-            jax.ShapeDtypeStruct((NC, 128, 128), bf16),
+            jax.ShapeDtypeStruct((128, 128), bf16),
+            jax.ShapeDtypeStruct((2, 128, 128), bf16),
         ),
-        in_specs=[ANY, VMEM, VMEM, VMEM],
-        out_specs=(VMEM, VMEM, VMEM),
+        in_specs=[ANY, ANY] + [VMEM] * 5,
+        out_specs=(VMEM, VMEM),
         scratch_shapes=[
+            pltpu.VMEM((3, 1024, 128), bf16), dma,
             pltpu.VMEM((CHIPS, 2, 2, 2, PIECE, 128), bf16),
             pltpu.VMEM((VOCAB, 128), bf16),
             pltpu.VMEM((2, 4, 64, 384), f32),
             pltpu.VMEM((3, 2, 64, 384), bf16), pltpu.VMEM((3, 2, 64, 384), bf16),
             pltpu.VMEM((2, 64, 384), bf16), pltpu.VMEM((2, 64, 384), bf16),
-            pltpu.VMEM((4, 2, 64, 384), bf16),
+            pltpu.VMEM((2, 4, 64, 384), bf16),
             pltpu.VMEM((NC, 1, 128), i32),
             pltpu.VMEM((NC, 128, 128), bf16),
             dma((2,)), dma((4,)), dma((4,)), dma((2, CHIPS)), dma((2, 2)),
             dma((2, CHIPS)), dma((2, CHIPS)), dma((2, CHIPS)), dma((2, CHIPS)),
             dma((3, 2)), dma((3, 2)), dma((2,)), dma((2,)), dma((3, 2)), dma((3, 2)),
             dma((NC - 1,)), dma((NC - 1,)), dma((NC - 1,)), dma((NC - 1,)),
-        ],
-        compiler_params=pltpu.CompilerParams(collective_id=0, has_side_effects=True, vmem_limit_bytes=LIMIT),
-        name="table",
-    )(embed, w, token_ids.reshape(1, 128), cotangent)
-    wide = pltpu.VMEM((1024, 128), f32)
-    mixed, pair = pl.pallas_call(
-        mix_kernel,
-        out_shape=(
-            jax.ShapeDtypeStruct((128, 128), bf16),
-            jax.ShapeDtypeStruct((2, 128, 128), f32),
-        ),
-        in_specs=[VMEM] * 7,
-        out_specs=(VMEM, VMEM),
-        scratch_shapes=[
             pltpu.VMEM((3, 136 * 8, 128), f32), pltpu.VMEM((3, 1024, 128), f32),
             wide, wide, wide, wide, wide,
             pltpu.VMEM((3, 1024, 128), f32), pltpu.VMEM((1024, 384), bf16),
             pltpu.VMEM((2, CHIPS, 128, 128), f32),
             pltpu.VMEM((2, CHIPS, 128, 128), bf16), pltpu.VMEM((2, CHIPS, 128, 128), bf16),
             pltpu.VMEM((2, CHIPS, 128, 128), bf16), pltpu.VMEM((2, CHIPS, 128, 128), bf16),
-            pltpu.VMEM((2, 128, 128), f32), pltpu.VMEM((2, 128, 128), f32),
+            pltpu.VMEM((2, 128, 128), bf16), pltpu.VMEM((2, 128, 128), bf16),
             dma((2, 4)), dma((2, 4)), dma((2, CHIPS)), dma((2, CHIPS)), dma((2,)), dma((2,)),
         ],
-        compiler_params=pltpu.CompilerParams(collective_id=1, has_side_effects=True, vmem_limit_bytes=LIMIT),
-        name="mix",
-    )(p, toks, cots, taps, rates, residues, w)
+        compiler_params=pltpu.CompilerParams(collective_id=0, has_side_effects=True, vmem_limit_bytes=LIMIT),
+        name="whole",
+    )(embed, w, token_ids.reshape(1, 128), cotangent, taps, rates, residues)
     return pl.pallas_call(
         last_kernel,
         out_shape=(jax.ShapeDtypeStruct((128, 128), bf16), jax.ShapeDtypeStruct((128, 128), bf16)),

time: 102 us -> 96.1 us (0.942)
  the two profiles are of different devices: /device:TPU:385 before, /device:TPU:384 now
where the time goes in v5:
time: 96.1 us; the launch traced here: 95.8 us
  Pallas kernels  95.2 us (99%)
    pallas_call x1, Pallas kernels, on_device(): pl.pallas_call(whole_kernel, out_shape=(jax.ShapeDtypeStruct((128, 128),...  93.7 us

profile of v5, /device:TPU:384, one launch (start us, length us, event | category | flops | bytes accessed | tf_op | source)
XLA Modules:
  0.0 95.8 jit_solution(3604777995891345013)
XLA Ops:
  0.6 93.7 %whole.1 = (bf16[128,128]{1,0:T(8,128)(2,1)}, bf16[2,128,128]{2,1,0:T(8,128)(2,1)}) custom-call(bf16[512,128]{1,0:T(8,128)(2,1)} %embed_ref.1, bf16[3,1024,128]{2,1,0:T(8,128)(2,1)} %bitcast.3, s32[1,128]{1,0:T(1,128)} %bitcast.5, bf16[128,128]{1,0:T(8,128)(2,1)} %cot_ref.1, f32[3,7,128]{2,1,0:T(8,128)} %bitcast.4, f32[16,128]{1,0:T(8,128)} %rates_ref.1, ...), custom_call_target="tpu_custom_call" | custom-call | tf_op jit(solution)/shard_map/whole/pallas_call | solution.py:588
  94.3 1.5 %last.1 = (bf16[128,128]{1,0:T(8,128)(2,1)}, bf16[128,128]{1,0:T(8,128)(2,1)}) custom-call(bf16[128,128]{1,0:T(8,128)(2,1)} %get-tuple-element.4.mixed_ref, bf16[2,128,128]{2,1,0:T(8,128)(2,1)} %get-tuple-element.5.pair_ref), custom_call_target="tpu_custom_call" | custom-call | tf_op jit(solution)/shard_map/last/pallas_call | solution.py:622

commit v6 on v5

--- a/solution.py
+++ b/solution.py
@@ -14,6 +14,7 @@
 NC = 8
 CHIPS = 16
 PIECE = 32
+FAR_FIRST = (10, 6, 14, 9, 11, 2, 8, 5, 7, 13, 15, 1, 3, 4, 12)
 VOCAB = 512
 MODES = 16
 TAPS = 7
@@ -22,11 +23,11 @@
 def place():
     f = lax.axis_index("fsdp")
     c = lax.axis_index("ctx")
-    return f // 16, (f // 4) % 4, (f // 2) % 2, f % 2, c
+    return lax.div(f, 16), lax.rem(lax.div(f, 4), 4), lax.rem(lax.div(f, 2), 2), lax.rem(f, 2), c
 
 
 def flat(x, y, h, k):
-    return (x % 4) * 16 + (y % 4) * 4 + h * 2 + k
+    return x * 16 + y * 4 + h * 2 + k
 
 
 def hail(devices):
@@ -48,8 +49,8 @@
 
 def build_table(
     friends, count, embed_ref, w_ref, w_copy, tok_ref, cot_ref,
-    emb, stage, acc, part_out, part_in, pair_out, pair_in, table, toks, cots,
-    local_sem, half_send, half_recv, scat_send, scat_recv, all_send, all_recv, core_send, core_recv,
+    emb, acc, part_out, part_in, pair_out, pair_in, table, toks, cots,
+    local_sem, scat_send, scat_recv, all_send, all_recv, core_send, core_recv,
     part_send, part_recv, pair_send, pair_recv, done_send, done_recv,
     cot_send, cot_recv, tok_send, tok_recv,
 ):
@@ -57,36 +58,33 @@
     x, y, h, k, c = place()
     me = flat(x, y, h, k)
     spot = x * 4 + y
-    mine = 2 * x + y // 2
-    yb = y % 2
+    lane = h * 2 + k
+    mine = 2 * x + lax.div(y, 2)
+    yb = lax.rem(y, 2)
     edge = jnp.where(mine < NC // 2, NC - 1, 0)
     source = mine == c
     gives = c == edge
     partner = flat(x, y, h, 1 - k)
-    other = flat(x, y, 1 - h, k)
-    q = c % 4
+    q = lax.rem(c, 4)
     base = c - q
-    across = (c + 4) % NC
-    group = [(me, base + (q + o) % 4) for o in range(1, 4)]
+    across = lax.rem(c + 4, NC)
+    group = [(me, base + lax.rem(q + o, 4)) for o in range(1, 4)]
+    first = flat(lax.div(c, 2), 2 * lax.rem(c, 2), 1 - h, k)
+    givers = [(first + 4 * row, jnp.where(c < NC // 2, NC - 1, 0)) for row in range(2)]
 
     def chip(i):
-        return flat(i // 4, i % 4, h, k)
+        return i * 4 + lane
+
+    def beside(o):
+        return lax.rem(spot + o, CHIPS)
 
     greet(
-        [((chip((spot + o) % CHIPS), c), None) for o in range(1, CHIPS)]
-        + [((partner, c), None)]
-        + [(d, None) for d in group + [(me, across)]]
-        + [((other, edge), source)]
-        + friends,
-        CHIPS + 4 + gives.astype(jnp.int32) + count,
+        friends
+        + [(d, None) for d in givers + [(me, across)] + group[::-1]]
+        + [((chip(beside(o)), c), None) for o in FAR_FIRST]
+        + [((partner, c), None)],
+        CHIPS + 4 + CHIPS * gives.astype(jnp.int32) + count,
     )
-
-    def half_copy(m):
-        rows = pl.ds(m * 128, 128)
-        return pltpu.make_async_remote_copy(
-            src_ref=embed_ref.at[rows], dst_ref=stage.at[rows], send_sem=half_send.at[m], recv_sem=half_recv.at[m],
-            device_id=(other, mine), device_id_type=MESH,
-        )
 
     def side(b):
         return h if b == 0 else 1 - h
@@ -94,50 +92,50 @@
     def scat_copy(b, i, row):
         rows = pl.ds(pl.multiple_of(i * PIECE, PIECE), PIECE)
         return pltpu.make_async_remote_copy(
-            src_ref=(embed_ref if b == 0 else stage).at[rows], dst_ref=emb.at[i, side(b), k, row],
+            src_ref=embed_ref.at[rows], dst_ref=emb.at[i, side(b), k, row],
             send_sem=scat_send.at[b, i], recv_sem=scat_recv.at[b, row], device_id=(chip(i), c), device_id_type=MESH,
         )
 
-    def own_copy(b):
-        rows = pl.ds(pl.multiple_of(spot * PIECE, PIECE), PIECE)
-        return pltpu.make_async_copy(
-            (embed_ref if b == 0 else stage).at[rows], emb.at[spot, side(b), k, yb], local_sem.at[b]
-        )
+    def give_copy(i):
+        rows = pl.ds(i * PIECE, PIECE)
+        return pltpu.make_async_remote_copy(
+            src_ref=embed_ref.at[rows], dst_ref=emb.at[i, h, k, yb], send_sem=scat_send.at[1, i],
+            recv_sem=scat_recv.at[1, yb], device_id=(i * 4 + (1 - h) * 2 + k, mine), device_id_type=MESH,
+        )
+
+    own_rows = pl.ds(pl.multiple_of(spot * PIECE, PIECE), PIECE)
+    own_copy = pltpu.make_async_copy(embed_ref.at[own_rows], emb.at[spot, h, k, yb], local_sem)
 
     def all_copy(b, o):
         return pltpu.make_async_remote_copy(
             src_ref=emb.at[spot, side(b), k], dst_ref=emb.at[spot, side(b), k], send_sem=all_send.at[b, o],
-            recv_sem=all_recv.at[b, o], device_id=(chip((spot + o) % CHIPS), c), device_id_type=MESH,
+            recv_sem=all_recv.at[b, o], device_id=(chip(beside(o)), c), device_id_type=MESH,
         )
 
     def core_copy(b, o):
-        i = (spot + CHIPS - o) % CHIPS
+        i = lax.rem(spot + CHIPS - o, CHIPS)
         return pltpu.make_async_remote_copy(
             src_ref=emb.at[i, side(b), k], dst_ref=emb.at[i, side(b), k], send_sem=core_send.at[b, o],
             recv_sem=core_recv.at[b, o], device_id=(partner, c), device_id_type=MESH,
         )
 
-    def each(first, last, body):
+    def each(first, last, body, unroll=1):
         def step(i, _):
             body(i)
             return 0
 
-        lax.fori_loop(first, last, step, 0)
+        lax.fori_loop(first, last, step, 0, unroll=unroll)
 
     @pl.when(gives)
     def _():
-        for m in range(4):
-            half_copy(m).start()
-
-    def scatter(b, o):
-        i = (spot + o) % CHIPS
-        scat_copy(b, i, yb).start()
+        for i in range(CHIPS):
+            give_copy(i).start()
 
     @pl.when(source)
     def _():
-        each(1, CHIPS, lambda o: scatter(0, o))
-        own_copy(0).start()
-        own_copy(0).wait()
+        own_copy.start()
+        each(1, CHIPS, lambda o: scat_copy(0, beside(o), yb).start(), 5)
+        own_copy.wait()
 
     extra = []
 
@@ -152,12 +150,16 @@
 
     def share(b):
         for row in range(2):
-
-            @pl.when(jnp.logical_not(jnp.logical_and(source, yb == row)))
-            def _():
+            if b == 0:
+
+                @pl.when(jnp.logical_not(jnp.logical_and(source, yb == row)))
+                def _():
+                    scat_copy(b, spot, row).wait_recv()
+
+            else:
                 scat_copy(b, spot, row).wait_recv()
 
-        each(1, CHIPS, lambda o: all_copy(b, o).start())
+        each(1, CHIPS, lambda o: all_copy(b, o).start(), 5)
         core_copy(b, 0).start()
 
     def gathered(b, o):
@@ -165,25 +167,12 @@
         core_copy(b, o).start()
 
     share(0)
-
-    @pl.when(source)
-    def _():
-        for m in range(4):
-            half_copy(m).wait_recv()
-            for i in range(m * 4, m * 4 + 4):
-
-                @pl.when(i != spot)
-                def _():
-                    scat_copy(1, i, yb).start()
-
-        own_copy(1).start()
-        own_copy(1).wait()
 
     for o in range(1, 4):
         spread(c, group[o - 1], o - 1)
     spread(c, (me, across), 3)
     share(1)
-    each(1, CHIPS, lambda o: gathered(0, o))
+    each(1, CHIPS, lambda o: gathered(0, o), 5)
     for copy in extra[6:8]:
         copy.wait_recv()
     for o in range(1, 4):
@@ -210,31 +199,31 @@
     w_copy.wait()
     for s in range(2):
         acc[s] = product(s, 0)
-    each(1, CHIPS, lambda o: gathered(1, o))
+    each(1, CHIPS, lambda o: gathered(1, o), 5)
     each(0, CHIPS, lambda o: core_copy(1, o).wait_recv())
 
     def part_copy(o, s):
         return pltpu.make_async_remote_copy(
             src_ref=part_out.at[o - 1, s], dst_ref=part_in.at[o - 1, s], send_sem=part_send.at[o - 1, s],
-            recv_sem=part_recv.at[o - 1, s], device_id=(me, base + (q + o) % 4), device_id_type=MESH,
+            recv_sem=part_recv.at[o - 1, s], device_id=(me, base + lax.rem(q + o, 4)), device_id_type=MESH,
         )
 
     def pair_copy(s):
         return pltpu.make_async_remote_copy(
             src_ref=pair_out.at[s], dst_ref=pair_in.at[s], send_sem=pair_send.at[s], recv_sem=pair_recv.at[s],
-            device_id=(me, (c + 4) % NC), device_id_type=MESH,
+            device_id=(me, across), device_id_type=MESH,
         )
 
     def done_copy(o, s):
         return pltpu.make_async_remote_copy(
             src_ref=table.at[s, q], dst_ref=table.at[s, q], send_sem=done_send.at[o - 1, s],
-            recv_sem=done_recv.at[o - 1, s], device_id=(me, base + (q + o) % 4), device_id_type=MESH,
+            recv_sem=done_recv.at[o - 1, s], device_id=(me, base + lax.rem(q + o, 4)), device_id_type=MESH,
         )
 
     for s in range(2):
         acc[s] = acc[s] + product(s, 1)
         for o in (3, 1, 2):
-            part_out[o - 1, s] = acc[s, (q + o) % 4].astype(bf16)
+            part_out[o - 1, s] = acc[s, lax.rem(q + o, 4)].astype(bf16)
             part_copy(o, s).start()
     for s in range(2):
         total = acc[s, q]
@@ -268,13 +257,12 @@
 
         @pl.when(source)
         def _():
-            for b in range(2):
-                each(1, CHIPS, lambda o: scat_copy(b, (spot + o) % CHIPS, yb).wait_send())
+            each(1, CHIPS, lambda o: scat_copy(0, beside(o), yb).wait_send())
 
         @pl.when(gives)
         def _():
-            for m in range(4):
-                half_copy(m).wait_send()
+            for i in range(CHIPS):
+                give_copy(i).wait_send()
 
         for s in range(2):
             pair_copy(s).wait_send()
@@ -412,7 +400,7 @@
 
     lax.fori_loop(0, 16, adjoint_rows, 0)
     for s in range(NC):
-        start = (c + s) % NC
+        start = lax.rem(c + s, NC)
         for g in range(3):
             lhs_ref[pl.ds(s * 128, 128), pl.ds(g * 128, 128)] = gz[g, pl.ds(start, 128, stride=8), :].astype(jnp.bfloat16)
 
@@ -424,8 +412,8 @@
     embed_ref, w_hbm, tok_ref, cot_ref, taps_ref, rates_ref, res_ref,
     mixed_ref, pair_ref,
     w_ref, w_sem,
-    emb, stage, acc, part_out, part_in, pair_out, pair_in, table, toks, cots,
-    local_sem, half_send, half_recv, scat_send, scat_recv, all_send, all_recv, swap_send, swap_recv,
+    emb, acc, part_out, part_in, pair_out, pair_in, table, toks, cots,
+    local_sem, scat_send, scat_recv, all_send, all_recv, swap_send, swap_recv,
     part_send, part_recv, pair_send, pair_recv, done_send, done_recv,
     cot_send, cot_recv, tok_send, tok_recv,
     z, filt, cot, drive, glong, lo, gd, gz, lhs_ref,
@@ -436,32 +424,33 @@
     w_copy.start()
     f32, bf16 = jnp.float32, jnp.bfloat16
     x, y, h, k, c = place()
-    x0, y0 = c // 2, (c % 2) * 2
-    dx, dy = (x - x0 + 4) % 4, (y - y0 + 4) % 4
+    x0, y0 = lax.div(c, 2), lax.rem(c, 2) * 2
+    dx, dy = lax.rem(x - x0 + 4, 4), lax.rem(y - y0 + 4, 4)
     partner = (flat(x, y, h, 1 - k), c)
     spot = x * 4 + y
-
-    def chip(o):
-        i = (spot + o) % CHIPS
-        return i // 4, i % 4
+    lane = h * 2 + k
+
+    def beside(o):
+        return lax.rem(spot + o, CHIPS)
 
     yb = jnp.where(jnp.logical_or(dy == 1, dy == 2), 1, 0)
     far = jnp.where(dy >= 2, 1, 0)
     step = jnp.where(dx < 2, dx + 2 * far, dx + 4 - 2 * far)
-    owner = [(flat(x0, y0 + yb, e, k), (c + step) % NC) for e in range(2)]
-    from_c = 2 * x + y // 2
-    back = (c - from_c + NC) % NC
-    back_x = jnp.where(back < 4, back % 2, 2 + back % 2)
-    back_far = jnp.where(back < 4, back // 2, 3 - back // 2)
-    back_y = jnp.where(y % 2 == 0, 3 * back_far, 1 + back_far)
-    givers = [(flat(x + back_x, (y // 2) * 2 + back_y, e, k), from_c) for e in range(2)]
+    owner = [(flat(x0, y0 + yb, e, k), lax.rem(c + step, NC)) for e in range(2)]
+    from_c = 2 * x + lax.div(y, 2)
+    back = lax.rem(c - from_c + NC, NC)
+    back_x = jnp.where(back < 4, lax.rem(back, 2), 2 + lax.rem(back, 2))
+    back_far = jnp.where(back < 4, lax.div(back, 2), 3 - lax.div(back, 2))
+    back_y = jnp.where(lax.rem(y, 2) == 0, 3 * back_far, 1 + back_far)
+    giver_x, giver_y = lax.rem(x + back_x, 4), lax.rem(lax.div(y, 2) * 2 + back_y, 4)
+    givers = [(flat(giver_x, giver_y, e, k), from_c) for e in range(2)]
     loop = jnp.logical_and(dx == 0, dy < 2)
     foreign = [jnp.logical_not(jnp.logical_and(loop, h == e)) for e in range(2)]
     finish = build_table(
         [(givers[e], foreign[e]) for e in range(2)], 2 - loop.astype(jnp.int32),
         embed_ref, w_ref, w_copy, tok_ref, cot_ref,
-        emb, stage, acc, part_out, part_in, pair_out, pair_in, table, toks, cots,
-        local_sem, half_send, half_recv, scat_send, scat_recv, all_send, all_recv, swap_send, swap_recv,
+        emb, acc, part_out, part_in, pair_out, pair_in, table, toks, cots,
+        local_sem, scat_send, scat_recv, all_send, all_recv, swap_send, swap_recv,
         part_send, part_recv, pair_send, pair_recv, done_send, done_recv,
         cot_send, cot_recv, tok_send, tok_recv,
     )
@@ -477,14 +466,14 @@
         )
 
     def slot(o):
-        cx, cy = chip(o)
-        return ((cx - x0 + 4) % 4) * 4 + (cy - y0 + 4) % 4
+        i = beside(o)
+        return lax.rem(lax.div(i, 4) + 4 - x0, 4) * 4 + lax.rem(lax.rem(i, 4) + 4 - y0, 4)
 
     def rest_copy(e, o):
         return pltpu.make_async_remote_copy(
             src_ref=rest_out.at[e, o], dst_ref=rest_in.at[e, o],
             send_sem=rest_send.at[e, o], recv_sem=rest_recv.at[e, o],
-            device_id=(flat(*chip(o), h, k), c), device_id_type=MESH,
+            device_id=(beside(o) * 4 + lane, c), device_id_type=MESH,
         )
 
     def last_copy(e):
@@ -532,7 +521,7 @@
             rest_copy(e, o).start()
             return 0
 
-        lax.fori_loop(1, CHIPS, give, 0)
+        lax.fori_loop(1, CHIPS, give, 0, unroll=3)
     for e in range(2):
 
         def take(o, both):
@@ -540,7 +529,7 @@
             return both + rest_in[e, o].astype(f32)
 
         home = dx * 4 + dy
-        both = lax.fori_loop(1, CHIPS, take, own[e, home] + core_in[e, home].astype(f32))
+        both = lax.fori_loop(1, CHIPS, take, own[e, home] + core_in[e, home].astype(f32), unroll=3)
         last_out[e] = both.astype(bf16)
 
         @pl.when(foreign[e])
@@ -596,14 +585,13 @@
         scratch_shapes=[
             pltpu.VMEM((3, 1024, 128), bf16), dma,
             pltpu.VMEM((CHIPS, 2, 2, 2, PIECE, 128), bf16),
-            pltpu.VMEM((VOCAB, 128), bf16),
             pltpu.VMEM((2, 4, 64, 384), f32),
             pltpu.VMEM((3, 2, 64, 384), bf16), pltpu.VMEM((3, 2, 64, 384), bf16),
             pltpu.VMEM((2, 64, 384), bf16), pltpu.VMEM((2, 64, 384), bf16),
             pltpu.VMEM((2, 4, 64, 384), bf16),
             pltpu.VMEM((NC, 1, 128), i32),
             pltpu.VMEM((NC, 128, 128), bf16),
-            dma((2,)), dma((4,)), dma((4,)), dma((2, CHIPS)), dma((2, 2)),
+            dma, dma((2, CHIPS)), dma((2, 2)),
             dma((2, CHIPS)), dma((2, CHIPS)), dma((2, CHIPS)), dma((2, CHIPS)),
             dma((3, 2)), dma((3, 2)), dma((2,)), dma((2,)), dma((3, 2)), dma((3, 2)),
             dma((NC - 1,)), dma((NC - 1,)), dma((NC - 1,)), dma((NC - 1,)),

time: 96.1 us -> 94.9 us (0.988)
  the two profiles are of different devices: /device:TPU:384 before, /device:TPU:1 now
where the time goes in v6:
time: 94.9 us; the launch traced here: 94.6 us
  Pallas kernels  94 us (99%)
    pallas_call x1, Pallas kernels, on_device(): pl.pallas_call(whole_kernel, out_shape=(jax.ShapeDtypeStruct((128, 128),...  92.5 us

profile of v6, /device:TPU:1, one launch (start us, length us, event | category | flops | bytes accessed | tf_op | source)
XLA Modules:
  0.0 94.6 jit_solution(6090274459742518962)
XLA Ops:
  0.6 92.5 %whole.1 = (bf16[128,128]{1,0:T(8,128)(2,1)}, bf16[2,128,128]{2,1,0:T(8,128)(2,1)}) custom-call(bf16[512,128]{1,0:T(8,128)(2,1)} %embed_ref.1, bf16[3,1024,128]{2,1,0:T(8,128)(2,1)} %bitcast.3, s32[1,128]{1,0:T(1,128)} %bitcast.5, bf16[128,128]{1,0:T(8,128)(2,1)} %cot_ref.1, f32[3,7,128]{2,1,0:T(8,128)} %bitcast.4, f32[16,128]{1,0:T(8,128)} %rates_ref.1, ...), custom_call_target="tpu_custom_call" | custom-call | tf_op jit(solution)/shard_map/whole/pallas_call | solution.py:577
  93.2 1.5 %last.1 = (bf16[128,128]{1,0:T(8,128)(2,1)}, bf16[128,128]{1,0:T(8,128)(2,1)}) custom-call(bf16[128,128]{1,0:T(8,128)(2,1)} %get-tuple-element.4.mixed_ref, bf16[2,128,128]{2,1,0:T(8,128)(2,1)} %get-tuple-element.5.pair_ref), custom_call_target="tpu_custom_call" | custom-call | tf_op jit(solution)/shard_map/last/pallas_call | solution.py:610

commit v7 on v6

--- a/solution.py
+++ b/solution.py
@@ -13,6 +13,7 @@
 LIMIT = 60 * 1024 * 1024
 NC = 8
 CHIPS = 16
+BLOCK = 8
 PIECE = 32
 FAR_FIRST = (10, 6, 14, 9, 11, 2, 8, 5, 7, 13, 15, 1, 3, 4, 12)
 VOCAB = 512
@@ -48,7 +49,7 @@
 
 
 def build_table(
-    friends, count, embed_ref, w_ref, w_copy, tok_ref, cot_ref,
+    friends, count, idle, embed_ref, w_ref, w_copy, tok_ref, cot_ref,
     emb, acc, part_out, part_in, pair_out, pair_in, table, toks, cots,
     local_sem, scat_send, scat_recv, all_send, all_recv, core_send, core_recv,
     part_send, part_recv, pair_send, pair_recv, done_send, done_recv,
@@ -225,6 +226,12 @@
         for o in (3, 1, 2):
             part_out[o - 1, s] = acc[s, lax.rem(q + o, 4)].astype(bf16)
             part_copy(o, s).start()
+    cots[c] = cot_ref[...]
+    toks[c] = tok_ref[...]
+    for i, copy in enumerate(extra):
+        if not 6 <= i < 8:
+            copy.wait_recv()
+    idle()
     for s in range(2):
         total = acc[s, q]
         for o in range(1, 4):
@@ -239,11 +246,6 @@
         for o in (3, 1, 2):
             done_copy(o, s).start()
 
-    cots[c] = cot_ref[...]
-    toks[c] = tok_ref[...]
-    for i, copy in enumerate(extra):
-        if not 6 <= i < 8:
-            copy.wait_recv()
     for s in range(2):
         for o in range(1, 4):
             done_copy(o, s).wait_recv()
@@ -281,77 +283,86 @@
     return jnp.where(row < 8 - by, pltpu.roll(value, 8 - by, 0), 0.0)
 
 
-def scan_modes(drive_at, out_ref, rates_ref, res_ref, backward):
+def scan_modes(src, out_ref, box, rates_ref, rd, hk, backward):
     row = lax.broadcasted_iota(jnp.int32, (8, 128), 0)
     shifted = shifted_down if backward else shifted_up
     length = 128
 
-    def spread(ref, m):
-        return jnp.broadcast_to(ref[m : m + 1, :], (8, 128))
-
-    def at(j):
+    def at(block, i):
+        j = block * BLOCK + i
         j = length - 1 - j if backward else j
         return pl.ds(pl.multiple_of(j * 8, 8), 8)
 
-    decay = [jnp.exp(-spread(rates_ref, m)) for m in range(MODES)]
-
-    def ends(j, state):
-        drive = drive_at(at(j))
-        return tuple(decay[m] * state[m] + drive for m in range(MODES))
+    def spread(factor):
+        whole = jnp.exp(-rates_ref[...] * float(factor))
+        return [jnp.broadcast_to(whole[m : m + 1, :], (8, 128)) for m in range(MODES)]
+
+    decay, jump = spread(1), spread(BLOCK)
+
+    def ends(block, state):
+        drive = [src[at(block, i), :] for i in range(BLOCK)]
+        out = []
+        for m in range(MODES):
+            value = drive[0]
+            for i in range(1, BLOCK):
+                value = decay[m] * value + drive[i]
+            box[block, m] = value
+            out.append(jump[m] * state[m] + value)
+        return tuple(out)
 
     zero = jnp.zeros((8, 128), jnp.float32)
-    state = lax.fori_loop(0, length, ends, (zero,) * MODES, unroll=4)
-    entering = []
-    for m in range(MODES):
-        rate = spread(rates_ref, m)
-        whole = state[m]
-        for by in (1, 2, 4):
-            whole = whole + jnp.exp(-rate * float(length * by)) * shifted(whole, by, row)
-        entering.append(shifted(whole, 1, row))
-    weight = [spread(res_ref, m) for m in range(MODES)]
-
-    def outs(j, state):
-        where = at(j)
-        drive = drive_at(where)
-        state = tuple(decay[m] * state[m] + drive for m in range(MODES))
-        terms = [weight[m] * state[m] for m in range(MODES)]
-        while len(terms) > 1:
-            terms = [a + b for a, b in zip(terms[::2], terms[1::2])]
-        out_ref[where, :] = terms[0]
-        return state
-
-    lax.fori_loop(0, length, outs, tuple(entering), unroll=4)
+    state = list(lax.fori_loop(0, length // BLOCK, ends, (zero,) * MODES))
+    for by in (1, 2, 4):
+        factor = spread(length * by)
+        state = [state[m] + factor[m] * shifted(state[m], by, row) for m in range(MODES)]
+    entering = tuple(shifted(state[m], 1, row) for m in range(MODES))
+
+    def outs(block, state):
+        drive = [src[at(block, i), :] for i in range(BLOCK)]
+        for i in range(BLOCK):
+            terms = [rd[i, m : m + 1, :] * state[m] for m in range(MODES)]
+            terms += [hk[i - n : i - n + 1, :] * drive[n] for n in range(i + 1)]
+            sums = terms[:4]
+            for n, term in enumerate(terms[4:]):
+                sums[n % 4] = sums[n % 4] + term
+            out_ref[at(block, i), :] = (sums[0] + sums[1]) + (sums[2] + sums[3])
+        return tuple(jump[m] * state[m] + box[block, m] for m in range(MODES))
+
+    lax.fori_loop(0, length // BLOCK, outs, entering)
+
+
+def prepare(toks, cots, rates_ref, res_ref, hot, cot, rd, hk):
+    lane = lax.broadcasted_iota(jnp.int32, (8, VOCAB), 1)
+    for s in range(NC):
+        cot[pl.ds(s, 128, stride=8), :] = cots[s].astype(jnp.float32)
+    for i in range(BLOCK):
+        rd[i] = res_ref[...] * jnp.exp(-rates_ref[...] * float(i + 1))
+        hk[i : i + 1, :] = jnp.sum(res_ref[...] * jnp.exp(-rates_ref[...] * float(i)), axis=0, keepdims=True)
+
+    def mark(i, ids):
+        rows = []
+        for j in range(0, 16, 2):
+            two = [jnp.where(ids[:, j + e : j + e + 1] == lane, 1.0, 0.0) for e in range(2)]
+            rows.append(jnp.concatenate(two, axis=0).astype(jnp.bfloat16))
+        hot[pl.ds(pl.multiple_of(i * 128, 128), 128), :] = jnp.concatenate(rows, axis=0)
+        return pltpu.roll(ids, 112, 1)
+
+    lax.fori_loop(0, 8, mark, jnp.concatenate([toks[i] for i in range(NC)], axis=0))
 
 
 def mix(
-    table, toks, cots, taps_ref, rates_ref, res_ref,
+    table, taps_ref, rates_ref,
     mixed_ref, lhs_ref,
-    z, filt, cot, drive, glong, lo, gd, gz,
+    hot, rd, hk, box, z, filt, cot, drive, glong, lo, gd, gz,
 ):
     c = lax.axis_index("ctx")
     halo = 8
     row = lax.broadcasted_iota(jnp.int32, (8, 128), 0)
-    lane = lax.broadcasted_iota(jnp.int32, (8, VOCAB), 1)
-
-    for s in range(NC):
-        cot[pl.ds(s, 128, stride=8), :] = cots[s].astype(jnp.float32)
-
-    ids = jnp.concatenate([toks[i] for i in range(NC)], axis=0)
     whole = table[...].reshape(VOCAB, 384)
-
-    def pick(i, ids):
-        rows = []
-        for j in range(0, 16, 2):
-            two = [jnp.where(ids[:, j + e : j + e + 1] == lane, 1.0, 0.0) for e in range(2)]
-            rows.append(jnp.concatenate(two, axis=0).astype(jnp.bfloat16))
-        hot = jnp.concatenate(rows, axis=0)
-        found = jnp.dot(hot, whole, preferred_element_type=jnp.float32)
-        start = pl.ds(pl.multiple_of((halo + i * 16) * 8, 128 // 2), 128)
+    for i in range(4):
+        found = jnp.dot(hot[i * 256 : (i + 1) * 256, :], whole, preferred_element_type=jnp.float32)
         for g in range(3):
-            z[g, start, :] = found[:, g * 128 : (g + 1) * 128]
-        return pltpu.roll(ids, 112, 1)
-
-    lax.fori_loop(0, 8, pick, ids)
+            z[g, pl.ds(halo * 8 + i * 256, 256), :] = found[:, g * 128 : (g + 1) * 128]
     for g in range(3):
         for d in range(1, TAPS):
             z[g, pl.ds((halo - d) * 8, 8), :] = shifted_up(z[g, pl.ds((halo + 128 - d) * 8, 8), :], 1, row)
@@ -370,8 +381,8 @@
         return 0
 
     lax.fori_loop(0, 16, filter_rows, 0)
-    scan_modes(lambda at: drive[at, :], lo, rates_ref, res_ref, False)
-    scan_modes(lambda at: glong[at, :], gd, rates_ref, res_ref, True)
+    scan_modes(drive, lo, box, rates_ref, rd, hk, False)
+    scan_modes(glong, gd, box, rates_ref, rd, hk, True)
 
     def grads(i, _):
         here = pl.ds(pl.multiple_of(i * 64, 64), 64)
@@ -416,7 +427,7 @@
     local_sem, scat_send, scat_recv, all_send, all_recv, swap_send, swap_recv,
     part_send, part_recv, pair_send, pair_recv, done_send, done_recv,
     cot_send, cot_recv, tok_send, tok_recv,
-    z, filt, cot, drive, glong, lo, gd, gz, lhs_ref,
+    hot, rd, hk, box, z, filt, cot, drive, glong, lo, gd, gz, lhs_ref,
     own, core_out, core_in, rest_out, rest_in, last_out, last_in,
     core_send, core_recv, rest_send, rest_recv, last_send, last_recv,
 ):
@@ -448,6 +459,7 @@
     foreign = [jnp.logical_not(jnp.logical_and(loop, h == e)) for e in range(2)]
     finish = build_table(
         [(givers[e], foreign[e]) for e in range(2)], 2 - loop.astype(jnp.int32),
+        lambda: prepare(toks, cots, rates_ref, res_ref, hot, cot, rd, hk),
         embed_ref, w_ref, w_copy, tok_ref, cot_ref,
         emb, acc, part_out, part_in, pair_out, pair_in, table, toks, cots,
         local_sem, scat_send, scat_recv, all_send, all_recv, swap_send, swap_recv,
@@ -455,8 +467,8 @@
         cot_send, cot_recv, tok_send, tok_recv,
     )
     mix(
-        table, toks, cots, taps_ref, rates_ref, res_ref, mixed_ref, lhs_ref,
-        z, filt, cot, drive, glong, lo, gd, gz,
+        table, taps_ref, rates_ref, mixed_ref, lhs_ref,
+        hot, rd, hk, box, z, filt, cot, drive, glong, lo, gd, gz,
     )
 
     def core_copy(e, a):
@@ -595,6 +607,8 @@
             dma((2, CHIPS)), dma((2, CHIPS)), dma((2, CHIPS)), dma((2, CHIPS)),
             dma((3, 2)), dma((3, 2)), dma((2,)), dma((2,)), dma((3, 2)), dma((3, 2)),
             dma((NC - 1,)), dma((NC - 1,)), dma((NC - 1,)), dma((NC - 1,)),
+            pltpu.VMEM((1024, VOCAB), bf16), pltpu.VMEM((BLOCK, MODES, 128), f32), pltpu.VMEM((BLOCK, 128), f32),
+            pltpu.VMEM((128 // BLOCK, MODES, 8, 128), f32),
             pltpu.VMEM((3, 136 * 8, 128), f32), pltpu.VMEM((3, 1024, 128), f32),
             wide, wide, wide, wide, wide,
             pltpu.VMEM((3, 1024, 128), f32), pltpu.VMEM((1024, 384), bf16),

time: 94.9 us -> 92.7 us (0.977)
  Pallas kernels: 94 us -> 91.8 us
    pallas_call x1, Pallas kernels: 92.5 us -> 90.3 us  [on_device(): pl.pallas_call(whole_kernel, out_shape=(jax.ShapeDtypeStruct((128, 128),...]
where the time goes in v7:
time: 92.7 us; the launch traced here: 92.4 us
  Pallas kernels  91.8 us (99%)
    pallas_call x1, Pallas kernels, on_device(): pl.pallas_call(whole_kernel, out_shape=(jax.ShapeDtypeStruct((128, 128),...  90.3 us

profile of v7, /device:TPU:1, one launch (start us, length us, event | category | flops | bytes accessed | tf_op | source)
XLA Modules:
  0.0 92.4 jit_solution(16796267192001610165)
XLA Ops:
  0.6 90.3 %whole.1 = (bf16[128,128]{1,0:T(8,128)(2,1)}, bf16[2,128,128]{2,1,0:T(8,128)(2,1)}) custom-call(bf16[512,128]{1,0:T(8,128)(2,1)} %embed_ref.1, bf16[3,1024,128]{2,1,0:T(8,128)(2,1)} %bitcast.3, s32[1,128]{1,0:T(1,128)} %bitcast.5, bf16[128,128]{1,0:T(8,128)(2,1)} %cot_ref.1, f32[3,7,128]{2,1,0:T(8,128)} %bitcast.4, f32[16,128]{1,0:T(8,128)} %rates_ref.1, ...), custom_call_target="tpu_custom_call" | custom-call | tf_op jit(solution)/shard_map/whole/pallas_call | solution.py:589
  90.9 1.5 %last.1 = (bf16[128,128]{1,0:T(8,128)(2,1)}, bf16[128,128]{1,0:T(8,128)(2,1)}) custom-call(bf16[128,128]{1,0:T(8,128)(2,1)} %get-tuple-element.4.mixed_ref, bf16[2,128,128]{2,1,0:T(8,128)(2,1)} %get-tuple-element.5.pair_ref), custom_call_target="tpu_custom_call" | custom-call | tf_op jit(solution)/shard_map/last/pallas_call | solution.py:624

commit v8 on v7

--- a/solution.py
+++ b/solution.py
@@ -27,6 +27,12 @@
     return lax.div(f, 16), lax.rem(lax.div(f, 4), 4), lax.rem(lax.div(f, 2), 2), lax.rem(f, 2), c
 
 
+def toward(x, y, o):
+    if isinstance(o, int):
+        return lax.rem(x + o // 4, 4) * 4 + lax.rem(y + o % 4, 4)
+    return lax.rem(x + lax.div(o, 4), 4) * 4 + lax.rem(y + lax.rem(o, 4), 4)
+
+
 def flat(x, y, h, k):
     return x * 16 + y * 4 + h * 2 + k
 
@@ -43,13 +49,8 @@
                 pl.semaphore_signal(barrier, inc=1, device_id=device, device_id_type=MESH)
 
 
-def greet(devices, count):
-    hail(devices)
-    pl.semaphore_wait(pltpu.get_barrier_semaphore(), count)
-
-
 def build_table(
-    friends, count, idle, embed_ref, w_ref, w_copy, tok_ref, cot_ref,
+    friends, count, idle, embed_ref, w_ref, fetches, tok_ref, cot_ref,
     emb, acc, part_out, part_in, pair_out, pair_in, table, toks, cots,
     local_sem, scat_send, scat_recv, all_send, all_recv, core_send, core_recv,
     part_send, part_recv, pair_send, pair_recv, done_send, done_recv,
@@ -77,15 +78,18 @@
         return i * 4 + lane
 
     def beside(o):
-        return lax.rem(spot + o, CHIPS)
-
-    greet(
+        return toward(x, y, o)
+
+    hail(
         friends
         + [(d, None) for d in givers + [(me, across)] + group[::-1]]
         + [((chip(beside(o)), c), None) for o in FAR_FIRST]
-        + [((partner, c), None)],
-        CHIPS + 4 + CHIPS * gives.astype(jnp.int32) + count,
+        + [((partner, c), None)]
     )
+    for fetch in fetches[::-1]:
+        fetch.start()
+    fetches[-1].wait()
+    pl.semaphore_wait(pltpu.get_barrier_semaphore(), CHIPS + 4 + CHIPS * gives.astype(jnp.int32) + count)
 
     def side(b):
         return h if b == 0 else 1 - h
@@ -97,8 +101,9 @@
             send_sem=scat_send.at[b, i], recv_sem=scat_recv.at[b, row], device_id=(chip(i), c), device_id_type=MESH,
         )
 
-    def give_copy(i):
-        rows = pl.ds(i * PIECE, PIECE)
+    def give_copy(o):
+        i = beside(o)
+        rows = pl.ds(pl.multiple_of(i * PIECE, PIECE), PIECE)
         return pltpu.make_async_remote_copy(
             src_ref=embed_ref.at[rows], dst_ref=emb.at[i, h, k, yb], send_sem=scat_send.at[1, i],
             recv_sem=scat_recv.at[1, yb], device_id=(i * 4 + (1 - h) * 2 + k, mine), device_id_type=MESH,
@@ -114,7 +119,7 @@
         )
 
     def core_copy(b, o):
-        i = lax.rem(spot + CHIPS - o, CHIPS)
+        i = lax.rem(x + 4 - lax.div(o, 4), 4) * 4 + lax.rem(y + 4 - lax.rem(o, 4), 4)
         return pltpu.make_async_remote_copy(
             src_ref=emb.at[i, side(b), k], dst_ref=emb.at[i, side(b), k], send_sem=core_send.at[b, o],
             recv_sem=core_recv.at[b, o], device_id=(partner, c), device_id_type=MESH,
@@ -129,13 +134,14 @@
 
     @pl.when(gives)
     def _():
-        for i in range(CHIPS):
-            give_copy(i).start()
+        for o in FAR_FIRST + (0,):
+            give_copy(o).start()
 
     @pl.when(source)
     def _():
         own_copy.start()
-        each(1, CHIPS, lambda o: scat_copy(0, beside(o), yb).start(), 5)
+        for o in FAR_FIRST:
+            scat_copy(0, beside(o), yb).start()
         own_copy.wait()
 
     extra = []
@@ -160,8 +166,9 @@
             else:
                 scat_copy(b, spot, row).wait_recv()
 
-        each(1, CHIPS, lambda o: all_copy(b, o).start(), 5)
-        core_copy(b, 0).start()
+        for o in FAR_FIRST:
+            all_copy(b, o).start()
+        core_copy(b, jnp.int32(0)).start()
 
     def gathered(b, o):
         all_copy(b, o).wait_recv()
@@ -197,58 +204,67 @@
         return total.reshape(4, 64, 384)
 
     each(0, CHIPS, lambda o: core_copy(0, o).wait_recv())
-    w_copy.wait()
+    fetches[0].wait()
     for s in range(2):
         acc[s] = product(s, 0)
     each(1, CHIPS, lambda o: gathered(1, o), 5)
     each(0, CHIPS, lambda o: core_copy(1, o).wait_recv())
 
-    def part_copy(o, s):
-        return pltpu.make_async_remote_copy(
-            src_ref=part_out.at[o - 1, s], dst_ref=part_in.at[o - 1, s], send_sem=part_send.at[o - 1, s],
-            recv_sem=part_recv.at[o - 1, s], device_id=(me, base + lax.rem(q + o, 4)), device_id_type=MESH,
-        )
-
-    def pair_copy(s):
-        return pltpu.make_async_remote_copy(
-            src_ref=pair_out.at[s], dst_ref=pair_in.at[s], send_sem=pair_send.at[s], recv_sem=pair_recv.at[s],
-            device_id=(me, across), device_id_type=MESH,
-        )
-
-    def done_copy(o, s):
-        return pltpu.make_async_remote_copy(
-            src_ref=table.at[s, q], dst_ref=table.at[s, q], send_sem=done_send.at[o - 1, s],
-            recv_sem=done_recv.at[o - 1, s], device_id=(me, base + lax.rem(q + o, 4)), device_id_type=MESH,
+    def rows_of(t):
+        return pl.ds(t % 2 * 32, 32)
+
+    def part_copy(o, t):
+        s, rows = t // 2, rows_of(t)
+        return pltpu.make_async_remote_copy(
+            src_ref=part_out.at[o - 1, s, rows], dst_ref=part_in.at[o - 1, s, rows], send_sem=part_send.at[o - 1, t],
+            recv_sem=part_recv.at[o - 1, t], device_id=group[o - 1], device_id_type=MESH,
+        )
+
+    def pair_copy(t):
+        s, rows = t // 2, rows_of(t)
+        return pltpu.make_async_remote_copy(
+            src_ref=pair_out.at[s, rows], dst_ref=pair_in.at[s, rows], send_sem=pair_send.at[t],
+            recv_sem=pair_recv.at[t], device_id=(me, across), device_id_type=MESH,
+        )
+
+    def done_copy(o, t):
+        s, rows = t // 2, rows_of(t)
+        return pltpu.make_async_remote_copy(
+            src_ref=table.at[s, q, rows], dst_ref=table.at[s, q, rows], send_sem=done_send.at[o - 1, t],
+            recv_sem=done_recv.at[o - 1, t], device_id=group[o - 1], device_id_type=MESH,
         )
 
     for s in range(2):
         acc[s] = acc[s] + product(s, 1)
-        for o in (3, 1, 2):
-            part_out[o - 1, s] = acc[s, lax.rem(q + o, 4)].astype(bf16)
-            part_copy(o, s).start()
-    cots[c] = cot_ref[...]
-    toks[c] = tok_ref[...]
+        for t in (2 * s, 2 * s + 1):
+            rows = rows_of(t)
+            for o in (3, 1, 2):
+                part_out[o - 1, s, rows, :] = acc[s, lax.rem(q + o, 4), rows, :].astype(bf16)
+                part_copy(o, t).start()
+    for fetch in fetches[1:-1]:
+        fetch.wait()
     for i, copy in enumerate(extra):
         if not 6 <= i < 8:
             copy.wait_recv()
     idle()
-    for s in range(2):
-        total = acc[s, q]
+    for t in range(4):
+        s, rows = t // 2, rows_of(t)
+        total = acc[s, q, rows, :]
         for o in range(1, 4):
-            part_copy(o, s).wait_recv()
-            total = total + part_in[o - 1, s].astype(f32)
-        acc[s, q] = total
-        pair_out[s] = total.astype(bf16)
-        pair_copy(s).start()
-    for s in range(2):
-        pair_copy(s).wait_recv()
-        table[s, q] = (acc[s, q] + pair_in[s].astype(f32)).astype(bf16)
+            part_copy(o, t).wait_recv()
+            total = total + part_in[o - 1, s, rows, :].astype(f32)
+        acc[s, q, rows, :] = total
+        pair_out[s, rows, :] = total.astype(bf16)
+        pair_copy(t).start()
+    for t in range(4):
+        s, rows = t // 2, rows_of(t)
+        pair_copy(t).wait_recv()
+        table[s, q, rows, :] = (acc[s, q, rows, :] + pair_in[s, rows, :].astype(f32)).astype(bf16)
         for o in (3, 1, 2):
-            done_copy(o, s).start()
-
-    for s in range(2):
+            done_copy(o, t).start()
+    for t in range(4):
         for o in range(1, 4):
-            done_copy(o, s).wait_recv()
+            done_copy(o, t).wait_recv()
 
     def finish():
         for copy in extra:
@@ -263,14 +279,14 @@
 
         @pl.when(gives)
         def _():
-            for i in range(CHIPS):
-                give_copy(i).wait_send()
-
-        for s in range(2):
-            pair_copy(s).wait_send()
+            for o in range(CHIPS):
+                give_copy(o).wait_send()
+
+        for t in range(4):
+            pair_copy(t).wait_send()
             for o in range(1, 4):
-                part_copy(o, s).wait_send()
-                done_copy(o, s).wait_send()
+                part_copy(o, t).wait_send()
+                done_copy(o, t).wait_send()
 
     return finish
 
@@ -420,9 +436,9 @@
 
 
 def whole_kernel(
-    embed_ref, w_hbm, tok_ref, cot_ref, taps_ref, rates_ref, res_ref,
+    embed_hbm, w_hbm, tok_ref, cot_ref, taps_hbm, rates_hbm, res_hbm,
     mixed_ref, pair_ref,
-    w_ref, w_sem,
+    embed_ref, w_ref, taps_ref, rates_ref, res_ref, fetch_sem,
     emb, acc, part_out, part_in, pair_out, pair_in, table, toks, cots,
     local_sem, scat_send, scat_recv, all_send, all_recv, swap_send, swap_recv,
     part_send, part_recv, pair_send, pair_recv, done_send, done_recv,
@@ -431,8 +447,6 @@
     own, core_out, core_in, rest_out, rest_in, last_out, last_in,
     core_send, core_recv, rest_send, rest_recv, last_send, last_recv,
 ):
-    w_copy = pltpu.make_async_copy(w_hbm, w_ref, w_sem)
-    w_copy.start()
     f32, bf16 = jnp.float32, jnp.bfloat16
     x, y, h, k, c = place()
     x0, y0 = lax.div(c, 2), lax.rem(c, 2) * 2
@@ -442,7 +456,7 @@
     lane = h * 2 + k
 
     def beside(o):
-        return lax.rem(spot + o, CHIPS)
+        return toward(x, y, o)
 
     yb = jnp.where(jnp.logical_or(dy == 1, dy == 2), 1, 0)
     far = jnp.where(dy >= 2, 1, 0)
@@ -457,10 +471,17 @@
     givers = [(flat(giver_x, giver_y, e, k), from_c) for e in range(2)]
     loop = jnp.logical_and(dx == 0, dy < 2)
     foreign = [jnp.logical_not(jnp.logical_and(loop, h == e)) for e in range(2)]
+    fetches = [
+        pltpu.make_async_copy(src, dst, fetch_sem.at[i])
+        for i, (src, dst) in enumerate((
+            (w_hbm, w_ref), (cot_ref, cots.at[c]), (tok_ref, toks.at[c]),
+            (taps_hbm, taps_ref), (rates_hbm, rates_ref), (res_hbm, res_ref), (embed_hbm, embed_ref),
+        ))
+    ]
     finish = build_table(
         [(givers[e], foreign[e]) for e in range(2)], 2 - loop.astype(jnp.int32),
         lambda: prepare(toks, cots, rates_ref, res_ref, hot, cot, rd, hk),
-        embed_ref, w_ref, w_copy, tok_ref, cot_ref,
+        embed_ref, w_ref, fetches, tok_ref, cot_ref,
         emb, acc, part_out, part_in, pair_out, pair_in, table, toks, cots,
         local_sem, scat_send, scat_recv, all_send, all_recv, swap_send, swap_recv,
         part_send, part_recv, pair_send, pair_recv, done_send, done_recv,
@@ -478,8 +499,7 @@
         )
 
     def slot(o):
-        i = beside(o)
-        return lax.rem(lax.div(i, 4) + 4 - x0, 4) * 4 + lax.rem(lax.rem(i, 4) + 4 - y0, 4)
+        return lax.rem(dx + o // 4, 4) * 4 + lax.rem(dy + o % 4, 4)
 
     def rest_copy(e, o):
         return pltpu.make_async_remote_copy(
@@ -527,13 +547,10 @@
         for a in range(4):
             core_copy(e, a).wait_recv()
 
-        def give(o, _):
+        for o in FAR_FIRST:
             a = slot(o)
             rest_out[e, o] = (own[e, a] + core_in[e, a].astype(f32)).astype(bf16)
             rest_copy(e, o).start()
-            return 0
-
-        lax.fori_loop(1, CHIPS, give, 0, unroll=3)
     for e in range(2):
 
         def take(o, both):
@@ -592,10 +609,11 @@
             jax.ShapeDtypeStruct((128, 128), bf16),
             jax.ShapeDtypeStruct((2, 128, 128), bf16),
         ),
-        in_specs=[ANY, ANY] + [VMEM] * 5,
+        in_specs=[ANY] * 7,
         out_specs=(VMEM, VMEM),
         scratch_shapes=[
-            pltpu.VMEM((3, 1024, 128), bf16), dma,
+            pltpu.VMEM((VOCAB, 128), bf16), pltpu.VMEM((3, 1024, 128), bf16), pltpu.VMEM((3, TAPS, 128), f32),
+            pltpu.VMEM((MODES, 128), f32), pltpu.VMEM((MODES, 128), f32), dma((7,)),
             pltpu.VMEM((CHIPS, 2, 2, 2, PIECE, 128), bf16),
             pltpu.VMEM((2, 4, 64, 384), f32),
             pltpu.VMEM((3, 2, 64, 384), bf16), pltpu.VMEM((3, 2, 64, 384), bf16),
@@ -605,7 +623,7 @@
             pltpu.VMEM((NC, 128, 128), bf16),
             dma, dma((2, CHIPS)), dma((2, 2)),
             dma((2, CHIPS)), dma((2, CHIPS)), dma((2, CHIPS)), dma((2, CHIPS)),
-            dma((3, 2)), dma((3, 2)), dma((2,)), dma((2,)), dma((3, 2)), dma((3, 2)),
+            dma((3, 4)), dma((3, 4)), dma((4,)), dma((4,)), dma((3, 4)), dma((3, 4)),
             dma((NC - 1,)), dma((NC - 1,)), dma((NC - 1,)), dma((NC - 1,)),
             pltpu.VMEM((1024, VOCAB), bf16), pltpu.VMEM((BLOCK, MODES, 128), f32), pltpu.VMEM((BLOCK, 128), f32),
             pltpu.VMEM((128 // BLOCK, MODES, 8, 128), f32),

time: 92.7 us -> 89 us (0.960)
  the two profiles are of different devices: /device:TPU:1 before, /device:TPU:5 now
where the time goes in v8:
time: 89 us; the launch traced here: 88.8 us
  Pallas kernels  88.2 us (99%)
    pallas_call x1, Pallas kernels, on_device(): pl.pallas_call(whole_kernel, out_shape=(jax.ShapeDtypeStruct((128, 128),...  86.7 us

profile of v8, /device:TPU:5, one launch (start us, length us, event | category | flops | bytes accessed | tf_op | source)
XLA Modules:
  0.0 88.8 jit_solution(18061551728612034174)
XLA Ops:
  0.6 86.7 %whole.1 = (bf16[128,128]{1,0:T(8,128)(2,1)}, bf16[2,128,128]{2,1,0:T(8,128)(2,1)}) custom-call(bf16[512,128]{1,0:T(8,128)(2,1)} %embed_hbm.1, bf16[3,1024,128]{2,1,0:T(8,128)(2,1)} %bitcast.3, s32[1,128]{1,0:T(1,128)} %bitcast.5, bf16[128,128]{1,0:T(8,128)(2,1)} %cot_ref.1, f32[3,7,128]{2,1,0:T(8,128)} %bitcast.4, f32[16,128]{1,0:T(8,128)} %rates_hbm.1, ...), custom_call_target="tpu_custom_call" | custom-call | tf_op jit(solution)/shard_map/whole/pallas_call | solution.py:606
  87.3 1.5 %last.1 = (bf16[128,128]{1,0:T(8,128)(2,1)}, bf16[128,128]{1,0:T(8,128)(2,1)}) custom-call(bf16[128,128]{1,0:T(8,128)(2,1)} %get-tuple-element.4.mixed_ref, bf16[2,128,128]{2,1,0:T(8,128)(2,1)} %get-tuple-element.5.pair_ref), custom_call_target="tpu_custom_call" | custom-call | tf_op jit(solution)/shard_map/last/pallas_call | solution.py:642

commit v9 on v8

--- a/solution.py
+++ b/solution.py
@@ -181,6 +181,7 @@
     spread(c, (me, across), 3)
     share(1)
     each(1, CHIPS, lambda o: gathered(0, o), 5)
+    each(1, CHIPS, lambda o: gathered(1, o), 5)
     for copy in extra[6:8]:
         copy.wait_recv()
     for o in range(1, 4):
@@ -207,8 +208,12 @@
     fetches[0].wait()
     for s in range(2):
         acc[s] = product(s, 0)
-    each(1, CHIPS, lambda o: gathered(1, o), 5)
     each(0, CHIPS, lambda o: core_copy(1, o).wait_recv())
+
+    far_first = [jnp.where(q < 2, 3 - i, 1 + i) for i in range(3)]
+
+    def member(o):
+        return me, base + lax.rem(q + o, 4)
 
     def rows_of(t):
         return pl.ds(t % 2 * 32, 32)
@@ -217,7 +222,7 @@
         s, rows = t // 2, rows_of(t)
         return pltpu.make_async_remote_copy(
             src_ref=part_out.at[o - 1, s, rows], dst_ref=part_in.at[o - 1, s, rows], send_sem=part_send.at[o - 1, t],
-            recv_sem=part_recv.at[o - 1, t], device_id=group[o - 1], device_id_type=MESH,
+            recv_sem=part_recv.at[o - 1, t], device_id=member(o), device_id_type=MESH,
         )
 
     def pair_copy(t):
@@ -231,14 +236,14 @@
         s, rows = t // 2, rows_of(t)
         return pltpu.make_async_remote_copy(
             src_ref=table.at[s, q, rows], dst_ref=table.at[s, q, rows], send_sem=done_send.at[o - 1, t],
-            recv_sem=done_recv.at[o - 1, t], device_id=group[o - 1], device_id_type=MESH,
+            recv_sem=done_recv.at[o - 1, t], device_id=member(o), device_id_type=MESH,
         )
 
     for s in range(2):
         acc[s] = acc[s] + product(s, 1)
         for t in (2 * s, 2 * s + 1):
             rows = rows_of(t)
-            for o in (3, 1, 2):
+            for o in far_first:
                 part_out[o - 1, s, rows, :] = acc[s, lax.rem(q + o, 4), rows, :].astype(bf16)
                 part_copy(o, t).start()
     for fetch in fetches[1:-1]:
@@ -260,7 +265,7 @@
         s, rows = t // 2, rows_of(t)
         pair_copy(t).wait_recv()
         table[s, q, rows, :] = (acc[s, q, rows, :] + pair_in[s, rows, :].astype(f32)).astype(bf16)
-        for o in (3, 1, 2):
+        for o in far_first:
             done_copy(o, t).start()
     for t in range(4):
         for o in range(1, 4):
@@ -544,6 +549,7 @@
             core_copy(e, a).start()
     for e in range(2):
         tile(e, k, to_own)
+    for e in range(2):
         for a in range(4):
             core_copy(e, a).wait_recv()
 

time: 89 us -> 90.1 us (1.012)
  the two profiles are of different devices: /device:TPU:5 before, /device:TPU:26 now
where the time goes in v9:
time: 90.1 us; the launch traced here: 89.9 us
  Pallas kernels  89.3 us (99%)
    pallas_call x1, Pallas kernels, on_device(): pl.pallas_call(whole_kernel, out_shape=(jax.ShapeDtypeStruct((128, 128),...  87.8 us

profile of v9, /device:TPU:26, one launch (start us, length us, event | category | flops | bytes accessed | tf_op | source)
XLA Modules:
  0.0 89.9 jit_solution(7983793322590491100)
XLA Ops:
  0.6 87.8 %whole.1 = (bf16[128,128]{1,0:T(8,128)(2,1)}, bf16[2,128,128]{2,1,0:T(8,128)(2,1)}) custom-call(bf16[512,128]{1,0:T(8,128)(2,1)} %embed_hbm.1, bf16[3,1024,128]{2,1,0:T(8,128)(2,1)} %bitcast.3, s32[1,128]{1,0:T(1,128)} %bitcast.5, bf16[128,128]{1,0:T(8,128)(2,1)} %cot_ref.1, f32[3,7,128]{2,1,0:T(8,128)} %bitcast.4, f32[16,128]{1,0:T(8,128)} %rates_hbm.1, ...), custom_call_target="tpu_custom_call" | custom-call | tf_op jit(solution)/shard_map/whole/pallas_call | solution.py:612
  88.4 1.5 %last.1 = (bf16[128,128]{1,0:T(8,128)(2,1)}, bf16[128,128]{1,0:T(8,128)(2,1)}) custom-call(bf16[128,128]{1,0:T(8,128)(2,1)} %get-tuple-element.4.mixed_ref, bf16[2,128,128]{2,1,0:T(8,128)(2,1)} %get-tuple-element.5.pair_ref), custom_call_target="tpu_custom_call" | custom-call | tf_op jit(solution)/shard_map/last/pallas_call | solution.py:648

commit v10 on v9

--- a/solution.py
+++ b/solution.py
@@ -181,7 +181,6 @@
     spread(c, (me, across), 3)
     share(1)
     each(1, CHIPS, lambda o: gathered(0, o), 5)
-    each(1, CHIPS, lambda o: gathered(1, o), 5)
     for copy in extra[6:8]:
         copy.wait_recv()
     for o in range(1, 4):
@@ -208,6 +207,7 @@
     fetches[0].wait()
     for s in range(2):
         acc[s] = product(s, 0)
+    each(1, CHIPS, lambda o: gathered(1, o), 5)
     each(0, CHIPS, lambda o: core_copy(1, o).wait_recv())
 
     far_first = [jnp.where(q < 2, 3 - i, 1 + i) for i in range(3)]
@@ -549,7 +549,6 @@
             core_copy(e, a).start()
     for e in range(2):
         tile(e, k, to_own)
-    for e in range(2):
         for a in range(4):
             core_copy(e, a).wait_recv()
 

time: 90.1 us -> 88.3 us (0.980)
  the two profiles are of different devices: /device:TPU:26 before, /device:TPU:1 now
where the time goes in v10:
time: 88.3 us; the launch traced here: 87.8 us
  Pallas kernels  87.1 us (99%)
    pallas_call x1, Pallas kernels, on_device(): pl.pallas_call(whole_kernel, out_shape=(jax.ShapeDtypeStruct((128, 128),...  85.6 us

profile of v10, /device:TPU:1, one launch (start us, length us, event | category | flops | bytes accessed | tf_op | source)
XLA Modules:
  0.0 87.8 jit_solution(14136920536787745098)
XLA Ops:
  0.6 85.6 %whole.1 = (bf16[128,128]{1,0:T(8,128)(2,1)}, bf16[2,128,128]{2,1,0:T(8,128)(2,1)}) custom-call(bf16[512,128]{1,0:T(8,128)(2,1)} %embed_hbm.1, bf16[3,1024,128]{2,1,0:T(8,128)(2,1)} %bitcast.3, s32[1,128]{1,0:T(1,128)} %bitcast.5, bf16[128,128]{1,0:T(8,128)(2,1)} %cot_ref.1, f32[3,7,128]{2,1,0:T(8,128)} %bitcast.4, f32[16,128]{1,0:T(8,128)} %rates_hbm.1, ...), custom_call_target="tpu_custom_call" | custom-call | tf_op jit(solution)/shard_map/whole/pallas_call | solution.py:611
  86.3 1.5 %last.1 = (bf16[128,128]{1,0:T(8,128)(2,1)}, bf16[128,128]{1,0:T(8,128)(2,1)}) custom-call(bf16[128,128]{1,0:T(8,128)(2,1)} %get-tuple-element.4.mixed_ref, bf16[2,128,128]{2,1,0:T(8,128)(2,1)} %get-tuple-element.5.pair_ref), custom_call_target="tpu_custom_call" | custom-call | tf_op jit(solution)/shard_map/last/pallas_call | solution.py:647
